TPU v7x, 32 devices: a whole 2x2x4 slice. The times are simulated.
32 devices in a mesh: gx: 8 (over y, x, core), gy: 4 (over z).
Axes of the slice: x: 2, y: 2, z: 4, core: 2. Of those that a mesh axis runs over, the one named last changes fastest.
Arguments:
- tracer_amounts: bfloat16 [2, 512, 512, 128], P(None, ('gx', 'gy')), may hold values from 0.099609375 to 3
- zonal_transit_ratio: float32 [2, 512, 512], P(None, 'gx', 'gy'), may hold values from -0.5 to 0.5
- meridional_transit_ratio: float32 [2, 512, 512], P(None, 'gx', 'gy'), may hold values from -0.45 to 0.45
- moisture_ratio: float32 [2, 512, 512], P(None, 'gx', 'gy'), may hold values from 0.2 to 0.9
- stratum_depths: float32 [2, 512, 512], P(None, 'gx', 'gy'), may hold values from 0.5 to 2
- sun_elevation_factor: float32 [512, 512], P('gx', 'gy'), may hold values from 0.2 to 1
- thermal_anomaly: float32 [2, 512, 512], P(None, 'gx', 'gy'), may hold values from -6 to 6
- particle_class_map: int32 [512, 512], P(('gx', 'gy')), may hold values from 0 to 7
- ground_cover_kind: int32 [512, 512], P(('gx', 'gy')), may hold values from 0 to 23
- arid_extinction_table: bfloat16 [128, 64], replicated, may hold values from 0 to 0.015625
- swelling_factors: bfloat16 [128, 64], replicated, may hold values from 0 to 0.00390625
- settling_velocities: float32 [24, 128], replicated, may hold values from 0.05 to 2
- arriving_irradiance: float32 [4], replicated, may hold values from 0.5 to 2
Outputs:
- updated_tracer_amounts: float32 [2, 512, 512, 128], P(None, ('gx', 'gy'))
- updated_thermal_anomaly: float32 [2, 512, 512], P(None, 'gx', 'gy')
All inputs are finite; a program needn't handle non-finite values.
Results may differ from a plain program's by a relative error of at most 0.00075.
Values may be sent and summed in bfloat16 or wider, within the bound.
A program may use at most 128 MiB of HBM per device.

v0:
```python
import jax
import jax.numpy as jnp
from jax import lax
from jax.sharding import PartitionSpec as P

SUB = 3
NBIN = 8
NW = 4


SPREAD_FACTOR = 0.2


def padded(cells, sides, width):
    for axis, dim in sides:
        count = lax.axis_size(axis)
        ends = count - 1
        head = lax.slice_in_dim(cells, 0, width, axis=dim)
        tail = lax.slice_in_dim(cells, cells.shape[dim] - width, cells.shape[dim], axis=dim)
        cells = jnp.concatenate(
            [
                lax.ppermute(tail, axis, [(i, (i + 1) % count) for i in range(ends)]),
                cells,
                lax.ppermute(head, axis, [((i + 1) % count, i) for i in range(ends)]),
            ],
            axis=dim,
        )
    return cells


def upwind(tracer, west_side, east_side, south_side, north_side, east_courant, north_courant):
    return (
        tracer
        - jnp.maximum(east_courant, 0.0) * (tracer - west_side)
        - jnp.minimum(east_courant, 0.0) * (east_side - tracer)
        - jnp.maximum(north_courant, 0.0) * (tracer - south_side)
        - jnp.minimum(north_courant, 0.0) * (north_side - tracer)
    )


def advance(widened, east_courant, north_courant):
    inner = widened[:, 1:-1]
    padded_y = jnp.pad(inner, ((0, 0), (0, 0), (1, 1), (0, 0)))
    return upwind(
        inner,
        widened[:, :-2],
        widened[:, 2:],
        padded_y[:, :, :-2],
        padded_y[:, :, 2:],
        east_courant,
        north_courant,
    )


def radiate(optical, cosine, sunlight):
    layers_count = optical.shape[0]
    wavelengths = optical.shape[1] // 2
    weights = sunlight.reshape((wavelengths,) + (1,) * (optical.ndim - 2))
    overhead = jnp.zeros_like(optical[0, :wavelengths])
    layers = [None] * layers_count
    for height in reversed(range(layers_count)):
        transmitted = jnp.exp(-overhead / cosine)
        layers[height] = cosine * jnp.sum(
            weights * optical[height, wavelengths:] * transmitted, axis=0
        )
        overhead = overhead + optical[height, :wavelengths]
    return jnp.stack(layers)


def per_device(
    tracer_amounts,
    zonal_transit_ratio,
    meridional_transit_ratio,
    moisture_ratio,
    stratum_depths,
    sun_elevation_factor,
    thermal_anomaly,
    particle_class_map,
    ground_cover_kind,
    arid_extinction_table,
    swelling_factors,
    settling_velocities,
    arriving_irradiance,
):
    tier_pile = thermal_anomaly.shape[0]
    strip_width = tracer_amounts.shape[1]
    species_count = tracer_amounts.shape[3]
    warmed_fringe_points = padded(
        thermal_anomaly.astype(jnp.bfloat16), (("gx", 1), ("gy", 2)), 1
    ).astype(thermal_anomaly.dtype)
    second_difference_map = (
        warmed_fringe_points[:, 2:, 1:-1]
        + warmed_fringe_points[:, :-2, 1:-1]
        + warmed_fringe_points[:, 1:-1, 2:]
        + warmed_fringe_points[:, 1:-1, :-2]
        - 4.0 * thermal_anomaly
    )
    fields = jnp.concatenate(
        [zonal_transit_ratio, meridional_transit_ratio, moisture_ratio, stratum_depths], axis=0
    )
    relayed = lax.all_to_all(fields, "gy", split_axis=1, concat_axis=2, tiled=True)
    moisture = relayed[2 * tier_pile : 3 * tier_pile]
    layer_depth = relayed[3 * tier_pile : 4 * tier_pile]
    widened = padded(tracer_amounts, ((("gx", "gy"), 1),), SUB).astype(jnp.float32)
    wind_rims = padded(relayed[: 2 * tier_pile], ((("gx", "gy"), 1),), SUB)
    span_width = strip_width + 2 * SUB
    first_column = lax.axis_index(("gx", "gy")) * strip_width - SUB
    grid_width = strip_width * lax.axis_size(("gx", "gy"))
    column_index = first_column + lax.iota(jnp.int32, span_width)
    inside = ((column_index >= 0) & (column_index < grid_width)).astype(jnp.float32)
    tracer = widened
    for substep in range(SUB):
        lower_edge = substep + 1
        upper_edge = span_width - substep - 1
        east_courant = wind_rims[:tier_pile, lower_edge:upper_edge][..., None]
        north_courant = wind_rims[tier_pile:, lower_edge:upper_edge][..., None]
        tracer = (
            advance(tracer, east_courant, north_courant)
            * inside[lower_edge:upper_edge][None, :, None, None]
        )
    land_count = settling_velocities.shape[0]
    one_hot = (ground_cover_kind[..., None] == lax.iota(jnp.int32, land_count)).astype(jnp.float32)
    loss_rate = jnp.dot(
        one_hot.reshape(-1, land_count), settling_velocities, precision=lax.Precision.HIGHEST
    ).reshape(strip_width, -1, species_count)
    loss_rate = loss_rate / layer_depth[0][..., None]
    updated_tracer_amounts = jnp.concatenate(
        [(tracer[0] / (1.0 + loss_rate))[None], tracer[1:]], axis=0
    )
    rounded = updated_tracer_amounts.astype(jnp.bfloat16)
    optics_table = jnp.concatenate([arid_extinction_table, swelling_factors], axis=1)
    projected = jnp.einsum(
        "lxys,sq->lqxy", rounded, optics_table, preferred_element_type=jnp.float32
    )
    projected = projected.reshape(tier_pile, 2, NBIN, 2 * NW, strip_width, -1)
    growth = moisture / (1.0 - moisture)
    combined = projected[:, 0] + growth[:, None, None] * projected[:, 1]
    bin_mask = (particle_class_map[None] == lax.iota(jnp.int32, NBIN)[:, None, None]).astype(
        jnp.float32
    )
    optical = jnp.sum(combined * bin_mask[None, :, None], axis=1) * layer_depth[:, None]
    payload = optical.reshape(tier_pile * 2 * NW, strip_width, -1)
    returned = lax.all_to_all(payload, "gy", split_axis=2, concat_axis=1, tiled=True)
    warming_tendency = radiate(
        returned.reshape(tier_pile, 2 * NW, returned.shape[1], returned.shape[2]),
        sun_elevation_factor,
        arriving_irradiance,
    )
    updated_thermal_anomaly = (
        thermal_anomaly + SPREAD_FACTOR * second_difference_map + warming_tendency
    )
    return (updated_tracer_amounts, updated_thermal_anomaly)


def solution(mesh):
    return jax.shard_map(
        per_device,
        mesh=mesh,
        in_specs=(
            P(None, ("gx", "gy"), None, None),
            P(None, "gx", "gy"),
            P(None, "gx", "gy"),
            P(None, "gx", "gy"),
            P(None, "gx", "gy"),
            P("gx", "gy"),
            P(None, "gx", "gy"),
            P(("gx", "gy"), None),
            P(("gx", "gy"), None),
            P(),
            P(),
            P(),
            P(),
        ),
        out_specs=(P(None, ("gx", "gy"), None, None), P(None, "gx", "gy")),
        check_vma=False,
    )
```

profile of v0, /device:TPU:4, one launch (start us, length us, event | category | flops | bytes accessed | tf_op | source)
XLA Modules:
  0.0 167.4 jit_solution(12056350276605661121)
XLA Ops:
  0.6 0.9 copy.36
  1.5 0.9 copy.37
  2.4 0.9 copy.38
  3.3 0.9 copy.39
  4.2 0.8 pad_maximum_fusion.1
  5.1 4.9 %all-to-all-start = ((f32[8,64,128]{2,0,1:T(8,128)}), f32[8,64,128]{2,0,1:T(8,128)S(1)}, u32[]{:S(2)}, u32[]{:S(2)}) async-start(f32[8,64,128]{2,0,1:T(8,128)} %pad_maximum_fusion.1), calls=%async_computation | async-start | bytes 524288 | tf_op jit(solution)/shard_map/all_to_all | solution.py:101
  9.9 2.4 %fusion.48 = (bf16[2,3,512,128]{3,2,1,0:T(8,128)(2,1)}, bf16[2,3,512,128]{3,2,1,0:T(8,128)(2,1)S(1)}) fusion(bf16[2,16,512,128]{3,2,1,0:T(8,128)(2,1)} %param.13), kind=kLoop, calls=%fused_computation.92 | loop fusion | bytes 3145728 | tf_op jit(solution)/shard_map/slice | solution.py:19
  12.3 3.9 %collective-permute-start = (bf16[2,3,512,128]{3,2,1,0:T(8,128)(2,1)}, bf16[2,3,512,128]{3,2,1,0:T(8,128)(2,1)S(1)}, u32[]{:S(2)}, u32[]{:S(2)}) collective-permute-start(bf16[2,3,512,128]{3,2,1,0:T(8,128)(2,1)} %get-tuple-element.4), channel_id=1, source_target_pairs={{0,1},{1,2},{2,3},{3,4},{4,5},{5,6},{6,7},{7,8},{8,9},{9,10},{10,1... | collective-permute-start | bytes 2359304 | tf_op jit(solution)/shard_map/ppermute | solution.py:22
  16.2 5.2 %collective-permute-start.1 = (bf16[2,3,512,128]{3,2,1,0:T(8,128)(2,1)S(1)}, bf16[2,3,512,128]{3,2,1,0:T(8,128)(2,1)S(1)}, u32[]{:S(2)}, u32[]{:S(2)}) collective-permute-start(bf16[2,3,512,128]{3,2,1,0:T(8,128)(2,1)S(1)} %get-tuple-element.5), channel_id=1, source_target_pairs={{1,0},{2,1},{3,2},{4,3},{5,4},{6,5},{7,6},{8,7},{9,8},{10,9},{11,1... | collective-permute-start | bytes 2359304 | tf_op jit(solution)/shard_map/ppermute | solution.py:24
  21.5 0.1 slice.167
  21.5 0.1 slice.175
  21.6 0.1 slice.183
  21.7 0.8 convert_element_type.31
  22.5 0.8 fusion.30
  23.3 0.2 copy.54
  23.5 0.7 fusion.49
  24.2 0.1 slice.158
  24.3 0.6 fusion.50
  24.9 1.9 %collective-permute-start.2 = (f32[4,3,512]{2,1,0:T(4,128)}, f32[4,3,512]{2,1,0:T(4,128)S(1)}, u32[]{:S(2)}, u32[]{:S(2)}) collective-permute-start(f32[4,3,512]{2,1,0:T(4,128)} %get-tuple-element.20), channel_id=1, source_target_pairs={{0,1},{1,2},{2,3},{3,4},{4,5},{5,6},{6,7},{7,8},{8,9},{9,10},{10,1... | collective-permute-start | bytes 73736 | tf_op jit(solution)/shard_map/ppermute | solution.py:22
  26.8 7.2 %collective-permute-start.3 = (f32[4,3,512]{2,1,0:T(4,128)}, f32[4,3,512]{2,1,0:T(4,128)S(1)}, u32[]{:S(2)}, u32[]{:S(2)}) collective-permute-start(f32[4,3,512]{2,1,0:T(4,128)} %get-tuple-element.21), channel_id=1, source_target_pairs={{1,0},{2,1},{3,2},{4,3},{5,4},{6,5},{7,6},{8,7},{9,8},{10,9},{11,1... | collective-permute-start | bytes 73736 | tf_op jit(solution)/shard_map/ppermute | solution.py:24
  34.1 0.9 slice.197
  34.9 0.6 subtract_divide_fusion
  35.6 1.5 max.43
  37.1 0.6 max.45
  37.7 0.6 min.43
  38.4 0.7 min.45
  39.0 0.7 mul.235
  39.7 15.7 %collective-permute-done.2 = f32[4,3,512]{2,1,0:T(4,128)S(1)} collective-permute-done((f32[4,3,512]{2,1,0:T(4,128)}, f32[4,3,512]{2,1,0:T(4,128)S(1)}, u32[]{:S(2)}, u32[]{:S(2)}) %collective-permute-start.2) | collective-permute-done | bytes 24608 | tf_op jit(solution)/shard_map/ppermute | solution.py:22
  55.4 0.7 slice_maximum_fusion.3
  56.2 0.7 slice_maximum_fusion.1
  56.9 3.5 %maximum_convert_fusion = f32[2,22,512,128]{3,2,1,0:T(8,128)S(1)} fusion(bf16[2,3,512,128]{3,2,1,0:T(8,128)(2,1)S(1)} %collective-permute-done.1, bf16[2,16,512,128]{3,2,1,0:T(8,128)(2,1)} %param.13, bf16[2,3,512,128]{3,2,1,0:T(8,128)(2,1)S(1)} %collective-permute-done), kind=kLoop, calls=%fused_computation.28 | loop fusion | flops 8650752 | bytes 17301504 | tf_op jit(solution)/shard_map/convert_element_type | solution.py:104
  60.5 4.7 %slice.203 = f32[2,20,512,128]{3,2,1,0:T(8,128)} slice(f32[2,22,512,128]{3,2,1,0:T(8,128)S(1)} %maximum_convert_fusion), slice={[0:2], [1:21], [0:512], [0:128]} | slice | bytes 20971520 | tf_op jit(solution)/shard_map/slice | solution.py:42
  65.2 15.3 %fusion.4 = f32[2,20,512,128]{3,2,1,0:T(8,128)} fusion(f32[2,20,512,128]{3,2,1,0:T(8,128)} %slice.203, f32[2,22,512,128]{3,2,1,0:T(8,128)S(1)} %maximum_convert_fusion, f32[20]{0:T(128)S(1)} %slice.167, f32[2,20,512]{2,1,0:T(8,128)S(1)} %copy-done.3, f32[2,20,512]{2,1,0:T(8,128)S(1)} %copy-done.4, f32[2,20,512]{2,1,0:T(8,128)S(1)} %get-tuple-element.17, ...), kind=kLoop, calls=%fused_computation.5 | loop fusion | flops 34078720 | bytes 42270800 | tf_op jit(solution)/shard_map/mul | solution.py:118
  80.5 3.7 %slice-done = f32[2,18,512,128]{3,2,1,0:T(8,128)S(1)} async-done(((f32[2,20,512,128]{3,2,1,0:T(8,128)}), f32[2,18,512,128]{3,2,1,0:T(8,128)S(1)}, s32[]{:S(2)}) %slice-start) | async-done | bytes 9437208 | tf_op jit(solution)/shard_map/slice | solution.py:42
  84.2 13.3 %fusion.11 = f32[2,18,512,128]{3,2,1,0:T(8,128)S(1)} fusion(f32[2,18,512,128]{3,2,1,0:T(8,128)S(1)} %slice-done, f32[2,20,512,128]{3,2,1,0:T(8,128)} %fusion.4, f32[18]{0:T(128)S(1)} %slice.175, f32[2,18,512]{2,1,0:T(8,128)} %get-tuple-element.14, f32[2,18,512]{2,1,0:T(8,128)} %get-tuple-element.15, f32[2,18,512]{2,1,0:T(8,128)S(1)} %get-tuple-element.13, ...), kind=kLoop, calls=%fused_computation.14 | loop fusion | flops 30670848 | bytes 38043720 | tf_op jit(solution)/shard_map/mul | solution.py:118
  97.5 0.6 slice.216
  98.1 0.2 copy-done.7
  98.4 10.9 %fusion.18 = f32[2,16,512,128]{3,2,1,0:T(8,128)} fusion(f32[2,16,512,128]{3,2,1,0:T(8,128)S(1)} %slice.216, f32[2,18,512,128]{3,2,1,0:T(8,128)S(1)} %fusion.11, f32[16]{0:T(128)S(1)} %slice.183, f32[2,16,512]{2,1,0:T(8,128)S(1)} %copy-done.10, f32[2,16,512]{2,1,0:T(8,128)S(1)} %copy-done.8, f32[2,16,512]{2,1,0:T(8,128)S(1)} %copy-done.9, ...), kind=kLoop, calls=%fused_computation.23 | loop fusion | flops 27262976 | bytes 33816640 | tf_op jit(solution)/shard_map/mul | solution.py:118
  109.3 3.4 %copy-done.2 = f32[2,16,512,128]{3,2,1,0:T(8,128)S(1)} copy-done((f32[2,16,512,128]{3,2,1,0:T(8,128)S(1)}, f32[2,16,512,128]{3,2,1,0:T(8,128)}, u32[]{:S(2)}) %copy-start.2) | copy-done | bytes 8388632
  112.7 6.7 %fusion.26 = f32[1,16,512,128]{3,2,1,0:T(8,128)} fusion(f32[2,16,512,128]{3,2,1,0:T(8,128)S(1)} %copy-done.2, f32[16,512]{1,0:T(8,128)S(1)} %bitcast.93, s32[16,512]{1,0:T(8,128)} %param.21, f32[24,128]{1,0:T(8,128)S(1)} %copy-done), kind=kOutput, calls=%fused_computation.37 | convolution fusion | flops 305332224 | bytes 8466432 | tf_op jit(solution)/shard_map/dot_general | solution.py:123
  119.4 3.5 %pad_maximum_fusion = f32[2,16,512,128]{3,2,1,0:T(8,128)S(1)} fusion(f32[1,16,512,128]{3,2,1,0:T(8,128)S(1)} %slice-done.1, f32[1,16,512,128]{3,2,1,0:T(8,128)} %fusion.26), kind=kLoop, calls=%fused_computation.27 | loop fusion | flops 2097152 | bytes 16777216 | tf_op jit(solution)/shard_map/concatenate | solution.py:127
  122.9 1.3 fusion.27
  124.2 2.1 %copy-done.1 = f32[2,16,512,128]{3,2,1,0:T(8,128)} copy-done((f32[2,16,512,128]{3,2,1,0:T(8,128)}, f32[2,16,512,128]{3,2,1,0:T(8,128)S(1)}, u32[]{:S(2)}) %copy-start.1) | copy-done | bytes 8388632
  126.3 1.4 fusion.24
  127.7 0.1 broadcast_multiply_fusion
  127.8 0.3 copy.43
  128.1 3.6 %copy.44 = f32[16,16,512]{1,0,2:T(8,128)} copy(f32[16,16,512]{2,1,0:T(8,128)S(1)} %bitcast.85) | data formatting | bytes 1048576 | tf_op jit(solution)/shard_map/mul | solution.py:141
  131.7 4.6 %reshape.118 = f32[4,1,32768]{2,1,0:T(1,128)} reshape(f32[512,16,16]{2,1,0:T(8,128)} %bitcast.83) | data formatting | bytes 1048576
  136.4 3.5 %all-to-all-start.1 = ((f32[4,1,32768]{2,1,0:T(1,128)}), f32[4,1,32768]{2,1,0:T(1,128)S(1)}, u32[]{:S(2)}, u32[]{:S(2)}) async-start(f32[4,1,32768]{2,1,0:T(1,128)} %reshape.118), calls=%async_computation.1 | async-start | bytes 1048576 | tf_op jit(solution)/shard_map/all_to_all | solution.py:143
  139.9 1.9 %collective-permute-start.4 = (bf16[2,1,128]{2,1,0:T(2,128)(2,1)S(1)}, bf16[2,1,128]{2,1,0:T(2,128)(2,1)S(1)}, u32[]{:S(2)}, u32[]{:S(2)}) collective-permute-start(bf16[2,1,128]{2,1,0:T(2,128)(2,1)S(1)} %get-tuple-element.26), channel_id=1, source_target_pairs={{0,4},{4,8},{8,12},{12,16},{16,20},{20,24},{24,28},{1,5},{5,9},{9,... | collective-permute-start | bytes 1544 | tf_op jit(solution)/shard_map/ppermute | solution.py:22
  141.8 4.7 %collective-permute-start.5 = (bf16[2,1,128]{2,1,0:T(2,128)(2,1)S(1)}, bf16[2,1,128]{2,1,0:T(2,128)(2,1)S(1)}, u32[]{:S(2)}, u32[]{:S(2)}) collective-permute-start(bf16[2,1,128]{2,1,0:T(2,128)(2,1)S(1)} %get-tuple-element.27), channel_id=1, source_target_pairs={{4,0},{8,4},{12,8},{16,12},{20,16},{24,20},{28,24},{5,1},{9,5},{13... | collective-permute-start | bytes 1544 | tf_op jit(solution)/shard_map/ppermute | solution.py:24
  146.5 1.1 collective-permute-done.5
  147.6 0.1 fusion.51
  147.7 3.9 %collective-permute-start.6 = (bf16[2,66,1]{2,1,0:T(8,128)(2,1)S(1)}, bf16[2,66,1]{2,1,0:T(8,128)(2,1)S(1)}, u32[]{:S(2)}, u32[]{:S(2)}) collective-permute-start(bf16[2,66,1]{2,1,0:T(8,128)(2,1)S(1)} %get-tuple-element.22), channel_id=1, source_target_pairs={{0,1},{1,2},{2,3},{4,5},{5,6},{6,7},{8,9},{9,10},{10,11},{12,13},{... | collective-permute-start | bytes 800 | tf_op jit(solution)/shard_map/ppermute | solution.py:22
  151.6 1.3 collective-permute-start.7
  152.9 0.3 collective-permute-done.6
  153.2 4.2 %collective-permute-done.7 = bf16[2,66,1]{2,1,0:T(8,128)(2,1)S(1)} collective-permute-done((bf16[2,66,1]{2,1,0:T(8,128)(2,1)S(1)}, bf16[2,66,1]{2,1,0:T(8,128)(2,1)S(1)}, u32[]{:S(2)}, u32[]{:S(2)}) %collective-permute-start.7) | collective-permute-done | bytes 296 | tf_op jit(solution)/shard_map/ppermute | solution.py:24
  157.4 0.1 maximum_convert_fusion.1
  157.6 0.5 broadcast.108
  158.1 2.2 %reduce = f32[4,32768]{1,0:T(4,128)S(1)} reduce(f32[4,1,32768]{2,1,0:T(1,128)S(1)} %all-to-all-done.1, f32[]{:T(128)} %broadcast.108), dimensions={1}, to_apply=%all_to_all.25.reduce_sub_computation | reduce | bytes 1048580 | tf_op jit(solution)/shard_map/all_to_all | solution.py:143
  160.3 3.4 %reshape.119 = f32[512,16,16]{2,1,0:T(8,128)} reshape(f32[4,32768]{1,0:T(4,128)S(1)} %reduce) | data formatting | bytes 1048576
  163.7 2.8 %copy.48 = f32[16,16,4,128]{3,2,1,0:T(4,128)S(1)} copy(f32[16,16,4,128]{1,0,3,2:T(8,128)} %bitcast.84) | data formatting | bytes 1048576 | tf_op jit(solution)/shard_map/all_to_all | solution.py:143
  166.6 0.1 fusion.39
  166.7 0.8 fusion.43
  (48 shorter events, 0.3 us)
Async XLA Ops:
  0.6 108.7 %copy-start = (f32[24,128]{1,0:T(8,128)S(1)}, f32[24,128]{1,0:T(8,128)}, u32[]{:S(2)}) copy-start(f32[24,128]{1,0:T(8,128)} %param.24) | copy-start | bytes 36868
  5.1 18.3 %all-to-all-start = ((f32[8,64,128]{2,0,1:T(8,128)}), f32[8,64,128]{2,0,1:T(8,128)S(1)}, u32[]{:S(2)}, u32[]{:S(2)}) async-start(f32[8,64,128]{2,0,1:T(8,128)} %pad_maximum_fusion.1), calls=%async_computation | async-start | bytes 524288 | tf_op jit(solution)/shard_map/all_to_all | solution.py:101
  12.3 44.6 %collective-permute-start = (bf16[2,3,512,128]{3,2,1,0:T(8,128)(2,1)}, bf16[2,3,512,128]{3,2,1,0:T(8,128)(2,1)S(1)}, u32[]{:S(2)}, u32[]{:S(2)}) collective-permute-start(bf16[2,3,512,128]{3,2,1,0:T(8,128)(2,1)} %get-tuple-element.4), channel_id=1, source_target_pairs={{0,1},{1,2},{2,3},{3,4},{4,5},{5,6},{6,7},{7,8},{8,9},{9,10},{10,1... | collective-permute-start | bytes 2359304 | tf_op jit(solution)/shard_map/ppermute | solution.py:22
  16.2 40.7 %collective-permute-start.1 = (bf16[2,3,512,128]{3,2,1,0:T(8,128)(2,1)S(1)}, bf16[2,3,512,128]{3,2,1,0:T(8,128)(2,1)S(1)}, u32[]{:S(2)}, u32[]{:S(2)}) collective-permute-start(bf16[2,3,512,128]{3,2,1,0:T(8,128)(2,1)S(1)} %get-tuple-element.5), channel_id=1, source_target_pairs={{1,0},{2,1},{3,2},{4,3},{5,4},{6,5},{7,6},{8,7},{9,8},{10,9},{11,1... | collective-permute-start | bytes 2359304 | tf_op jit(solution)/shard_map/ppermute | solution.py:24
  24.9 30.5 %collective-permute-start.2 = (f32[4,3,512]{2,1,0:T(4,128)}, f32[4,3,512]{2,1,0:T(4,128)S(1)}, u32[]{:S(2)}, u32[]{:S(2)}) collective-permute-start(f32[4,3,512]{2,1,0:T(4,128)} %get-tuple-element.20), channel_id=1, source_target_pairs={{0,1},{1,2},{2,3},{3,4},{4,5},{5,6},{6,7},{7,8},{8,9},{9,10},{10,1... | collective-permute-start | bytes 73736 | tf_op jit(solution)/shard_map/ppermute | solution.py:22
  26.8 28.6 %collective-permute-start.3 = (f32[4,3,512]{2,1,0:T(4,128)}, f32[4,3,512]{2,1,0:T(4,128)S(1)}, u32[]{:S(2)}, u32[]{:S(2)}) collective-permute-start(f32[4,3,512]{2,1,0:T(4,128)} %get-tuple-element.21), channel_id=1, source_target_pairs={{1,0},{2,1},{3,2},{4,3},{5,4},{6,5},{7,6},{8,7},{9,8},{10,9},{11,1... | collective-permute-start | bytes 73736 | tf_op jit(solution)/shard_map/ppermute | solution.py:24
  60.4 4.7 %copy-start.3 = (f32[2,20,512]{2,1,0:T(8,128)S(1)}, f32[2,20,512]{2,1,0:T(8,128)}, u32[]{:S(2)}) copy-start(f32[2,20,512]{2,1,0:T(8,128)} %get-tuple-element.18) | copy-start | bytes 245764
  60.5 4.7 %copy-start.4 = (f32[2,20,512]{2,1,0:T(8,128)S(1)}, f32[2,20,512]{2,1,0:T(8,128)}, u32[]{:S(2)}) copy-start(f32[2,20,512]{2,1,0:T(8,128)} %get-tuple-element.19) | copy-start | bytes 245764
  80.5 3.7 %slice-start = ((f32[2,20,512,128]{3,2,1,0:T(8,128)}), f32[2,18,512,128]{3,2,1,0:T(8,128)S(1)}, s32[]{:S(2)}) async-start(f32[2,20,512,128]{3,2,1,0:T(8,128)} %fusion.4), calls=%async_computation.2 | async-start | bytes 18874368 | tf_op jit(solution)/shard_map/slice | solution.py:42
  97.5 0.8 copy-start.7
  97.5 0.9 copy-start.8
  97.5 0.9 copy-start.9
  97.5 0.9 copy-start.10
  109.3 3.4 %copy-start.2 = (f32[2,16,512,128]{3,2,1,0:T(8,128)S(1)}, f32[2,16,512,128]{3,2,1,0:T(8,128)}, u32[]{:S(2)}) copy-start(f32[2,16,512,128]{3,2,1,0:T(8,128)} %fusion.18) | copy-start | bytes 25165828
  112.7 6.7 %slice-start.1 = ((f32[2,16,512,128]{3,2,1,0:T(8,128)}), f32[1,16,512,128]{3,2,1,0:T(8,128)S(1)}, s32[]{:S(2)}) async-start(f32[2,16,512,128]{3,2,1,0:T(8,128)} %fusion.18), calls=%async_computation.3 | async-start | bytes 8388608 | tf_op jit(solution)/shard_map/slice | solution.py:128
  119.4 3.5 %copy-start.13 = (bf16[128,64]{0,1:T(8,128)(2,1)S(1)}, bf16[128,64]{0,1:T(8,128)(2,1)}, u32[]{:S(2)}) copy-start(bf16[128,64]{0,1:T(8,128)(2,1)} %param.23) | copy-start | bytes 49156
  119.4 3.5 %copy-start.14 = (bf16[128,64]{0,1:T(8,128)(2,1)S(1)}, bf16[128,64]{0,1:T(8,128)(2,1)}, u32[]{:S(2)}) copy-start(bf16[128,64]{0,1:T(8,128)(2,1)} %param.22) | copy-start | bytes 49156
  122.9 3.4 %copy-start.1 = (f32[2,16,512,128]{3,2,1,0:T(8,128)}, f32[2,16,512,128]{3,2,1,0:T(8,128)S(1)}, u32[]{:S(2)}) copy-start(f32[2,16,512,128]{3,2,1,0:T(8,128)S(1)} %pad_maximum_fusion) | copy-start | bytes 25165828
  122.9 3.4 %copy-start.6 = (f32[2,16,512]{2,1,0:T(8,128)S(1)}, f32[2,16,512]{2,1,0:T(8,128)}, u32[]{:S(2)}) copy-start(f32[2,16,512]{2,1,0:T(8,128)} %subtract_divide_fusion) | copy-start | bytes 196612
  126.3 1.4 copy-start.12
  127.7 25.2 %copy-start.5 = (f32[64,128]{1,0:T(8,128)S(1)}, f32[64,128]{1,0:T(8,128)}, u32[]{:S(2)}) copy-start(f32[64,128]{1,0:T(8,128)} %param.18) | copy-start | bytes 98308
  131.7 34.8 %copy-start.15 = (f32[4]{0:T(128)S(1)}, f32[4]{0:T(128)}, u32[]{:S(2)}) copy-start(f32[4]{0:T(128)} %param.25) | copy-start | bytes 52
  131.7 35.0 %copy-start.11 = (f32[2,64,128]{2,1,0:T(8,128)S(1)}, f32[2,64,128]{2,1,0:T(8,128)}, u32[]{:S(2)}) copy-start(f32[2,64,128]{2,1,0:T(8,128)} %param.19) | copy-start | bytes 196612
  136.4 21.2 %all-to-all-start.1 = ((f32[4,1,32768]{2,1,0:T(1,128)}), f32[4,1,32768]{2,1,0:T(1,128)S(1)}, u32[]{:S(2)}, u32[]{:S(2)}) async-start(f32[4,1,32768]{2,1,0:T(1,128)} %reshape.118), calls=%async_computation.1 | async-start | bytes 1048576 | tf_op jit(solution)/shard_map/all_to_all | solution.py:143
  139.9 6.7 %collective-permute-start.4 = (bf16[2,1,128]{2,1,0:T(2,128)(2,1)S(1)}, bf16[2,1,128]{2,1,0:T(2,128)(2,1)S(1)}, u32[]{:S(2)}, u32[]{:S(2)}) collective-permute-start(bf16[2,1,128]{2,1,0:T(2,128)(2,1)S(1)} %get-tuple-element.26), channel_id=1, source_target_pairs={{0,4},{4,8},{8,12},{12,16},{16,20},{20,24},{24,28},{1,5},{5,9},{9,... | collective-permute-start | bytes 1544 | tf_op jit(solution)/shard_map/ppermute | solution.py:22
  141.8 5.8 %collective-permute-start.5 = (bf16[2,1,128]{2,1,0:T(2,128)(2,1)S(1)}, bf16[2,1,128]{2,1,0:T(2,128)(2,1)S(1)}, u32[]{:S(2)}, u32[]{:S(2)}) collective-permute-start(bf16[2,1,128]{2,1,0:T(2,128)(2,1)S(1)} %get-tuple-element.27), channel_id=1, source_target_pairs={{4,0},{8,4},{12,8},{16,12},{20,16},{24,20},{28,24},{5,1},{9,5},{13... | collective-permute-start | bytes 1544 | tf_op jit(solution)/shard_map/ppermute | solution.py:24
  147.7 5.5 %collective-permute-start.6 = (bf16[2,66,1]{2,1,0:T(8,128)(2,1)S(1)}, bf16[2,66,1]{2,1,0:T(8,128)(2,1)S(1)}, u32[]{:S(2)}, u32[]{:S(2)}) collective-permute-start(bf16[2,66,1]{2,1,0:T(8,128)(2,1)S(1)} %get-tuple-element.22), channel_id=1, source_target_pairs={{0,1},{1,2},{2,3},{4,5},{5,6},{6,7},{8,9},{9,10},{10,11},{12,13},{... | collective-permute-start | bytes 800 | tf_op jit(solution)/shard_map/ppermute | solution.py:22
  151.6 5.9 %collective-permute-start.7 = (bf16[2,66,1]{2,1,0:T(8,128)(2,1)S(1)}, bf16[2,66,1]{2,1,0:T(8,128)(2,1)S(1)}, u32[]{:S(2)}, u32[]{:S(2)}) collective-permute-start(bf16[2,66,1]{2,1,0:T(8,128)(2,1)S(1)} %get-tuple-element.23), channel_id=1, source_target_pairs={{1,0},{2,1},{3,2},{5,4},{6,5},{7,6},{9,8},{10,9},{11,10},{13,12},{... | collective-permute-start | bytes 800 | tf_op jit(solution)/shard_map/ppermute | solution.py:24
where the time goes:
time: 169 us; the launch traced here: 167 us
  other arithmetic  56.4 us (33%)
  local copies, waits for them, and re-layouts  42.3 us (25%)
  starting transfers between devices  38.4 us (23%)
  waiting for transfers between devices  21.4 us (13%)
  matrix products  7.92 us (5%)
    mul x3, other arithmetic, per_device(): advance(tracer, east_courant, north_courant)  39.5 us
    ppermute x4, starting transfers between devices, padded(): lax.ppermute(head, axis, [((i + 1) % count, i) for i in range(ends)])  18.5 us
    unnamed x39, local copies, waits for them, and re-layouts  17.5 us
    ppermute x4, waiting for transfers between devices, padded(): lax.ppermute(tail, axis, [(i, (i + 1) % count) for i in range(ends)])  16 us
    ppermute x4, starting transfers between devices, padded(): lax.ppermute(tail, axis, [(i, (i + 1) % count) for i in range(ends)])  11.6 us
    slice x4, local copies, waits for them, and re-layouts, advance(): inner = widened[:, 1:-1]  8.95 us
    dot_general x1, matrix products, per_device(): jnp.dot(one_hot.reshape(-1, land_count), settling_velocities, precision=l...  6.66 us
    ppermute x4, waiting for transfers between devices, padded(): lax.ppermute(head, axis, [((i + 1) % count, i) for i in range(ends)])  5.33 us
  transfers between devices with their start and end apart: 10, of which 4 were waited for; matrix products, arithmetic and copies ran while one was open for 8% of the time, Pallas kernels for 0%

commit v1 on v0

v1 whole, which is shorter than its diff:
```python
import functools

import jax
import jax.numpy as jnp
from jax import lax
from jax.experimental import pallas as pl
from jax.experimental.pallas import tpu as pltpu
from jax.sharding import PartitionSpec as P

SUB = 3
NBIN = 8
NW = 4
SPREAD_FACTOR = 0.2
PAD = 8
LAND_ROWS = 32
MESH = pl.DeviceIdType.MESH
VMEM_SPEC = pl.BlockSpec(memory_space=pltpu.VMEM)
SMEM_SPEC = pl.BlockSpec(memory_space=pltpu.SMEM)


def greet(gx_count, gy_count, reach):
    gx = lax.axis_index("gx")
    gy = lax.axis_index("gy")
    barrier = pltpu.get_barrier_semaphore()
    for dx in range(-reach, reach + 1):
        for dy in range(gy_count):
            if dx == 0 and dy == 0:
                continue
            pl.semaphore_signal(
                barrier,
                inc=1,
                device_id=(
                    lax.rem(gx + dx + gx_count, gx_count),
                    lax.rem(gy + dy, gy_count),
                ),
                device_id_type=MESH,
            )
    pl.semaphore_wait(barrier, (2 * reach + 1) * gy_count - 1)


def fields_kernel(
    gx_count, gy_count, width,
    fields, sun, fringe,
    strip, rim, strip_sun, fringe_in,
    send_a, recv_a, send_s, recv_s, send_r, recv_r, send_f, recv_f,
):
    gx = lax.axis_index("gx")
    gy = lax.axis_index("gy")
    span = width + 2 * SUB
    tile_x = width * gy_count
    tile_y = fields.shape[2]
    right = lax.rem(gx + 1, gx_count)
    left = lax.rem(gx + gx_count - 1, gx_count)
    up = lax.rem(gy + 1, gy_count)
    down = lax.rem(gy + gy_count - 1, gy_count)
    greet(gx_count, gy_count, 1)
    mine = pl.ds(pl.multiple_of(gy * tile_y, tile_y), tile_y)

    def rims(side):
        lo = tile_x if side == 0 else SUB
        return pltpu.make_async_remote_copy(
            src_ref=fields.at[pl.ds(lo, SUB)],
            dst_ref=rim.at[side, :, :, mine],
            send_sem=send_r.at[side],
            recv_sem=recv_r.at[gy],
            device_id=((right, 0) if side == 0 else (left, gy_count - 1)),
            device_id_type=MESH,
        )

    def slab(peer):
        return pltpu.make_async_remote_copy(
            src_ref=fields.at[pl.ds(peer * width, span)],
            dst_ref=strip.at[:, :, mine],
            send_sem=send_a.at[peer],
            recv_sem=recv_a.at[gy],
            device_id=(gx, peer),
            device_id_type=MESH,
        )

    def sunny(peer):
        return pltpu.make_async_remote_copy(
            src_ref=sun.at[pl.ds(peer * width, width)],
            dst_ref=strip_sun.at[:, mine],
            send_sem=send_s.at[peer],
            recv_sem=recv_s.at[gy],
            device_id=(gx, peer),
            device_id_type=MESH,
        )

    targets = ((left, gy), (right, gy), (gx, down), (gx, up))
    edges = [
        pltpu.make_async_remote_copy(
            src_ref=fringe.at[k],
            dst_ref=fringe_in.at[k],
            send_sem=send_f.at[k],
            recv_sem=recv_f.at[k],
            device_id=targets[k],
            device_id_type=MESH,
        )
        for k in range(4)
    ]
    for peer in range(gy_count):
        @pl.when(gy != peer)
        def _(peer=peer):
            slab(peer).start()
            sunny(peer).start()
    for side in range(2):
        rims(side).start()
    for edge in edges:
        edge.start()
    strip[:, :, mine] = fields[pl.ds(gy * width, span)]
    strip_sun[:, mine] = sun[pl.ds(pl.multiple_of(gy * width, width), width), :]
    for edge in edges:
        edge.wait()
    for side in range(2):
        rims(side).wait_send()
    for peer in range(gy_count):
        @pl.when(gy != peer)
        def _(peer=peer):
            slab(peer).wait_send()
            sunny(peer).wait_send()
            theirs = pl.ds(peer * tile_y, tile_y)
            pltpu.make_async_remote_copy(
                src_ref=fields.at[pl.ds(0, span)],
                dst_ref=strip.at[:, :, theirs],
                send_sem=send_a.at[peer],
                recv_sem=recv_a.at[peer],
                device_id=(gx, peer),
                device_id_type=MESH,
            ).wait_recv()
            pltpu.make_async_remote_copy(
                src_ref=sun.at[pl.ds(0, width)],
                dst_ref=strip_sun.at[:, theirs],
                send_sem=send_s.at[peer],
                recv_sem=recv_s.at[peer],
                device_id=(gx, peer),
                device_id_type=MESH,
            ).wait_recv()
    for side, owner, source in ((0, 0, left), (1, gy_count - 1, right)):
        @pl.when(gy == owner)
        def _(side=side, source=source):
            for peer in range(gy_count):
                pltpu.make_async_remote_copy(
                    src_ref=fields.at[pl.ds(0, SUB)],
                    dst_ref=rim.at[side, :, :, pl.ds(peer * tile_y, tile_y)],
                    send_sem=send_r.at[side],
                    recv_sem=recv_r.at[peer],
                    device_id=(source, peer),
                    device_id_type=MESH,
                ).wait_recv()


def return_kernel(
    gx_count, gy_count, width, heat, base, out, tile, send_sem, recv_sem
):
    gx = lax.axis_index("gx")
    gy = lax.axis_index("gy")
    tile_y = base.shape[2]
    greet(gx_count, gy_count, 0)

    def slab(peer):
        return pltpu.make_async_remote_copy(
            src_ref=heat.at[:, :, pl.ds(peer * tile_y, tile_y)],
            dst_ref=tile.at[pl.ds(gy * width, width)],
            send_sem=send_sem.at[peer],
            recv_sem=recv_sem.at[gy],
            device_id=(gx, peer),
            device_id_type=MESH,
        )

    for peer in range(gy_count):
        @pl.when(gy != peer)
        def _(peer=peer):
            slab(peer).start()
    mine = pl.ds(pl.multiple_of(gy * tile_y, tile_y), tile_y)
    tile[pl.ds(gy * width, width)] = heat[:, :, mine]
    for peer in range(gy_count):
        @pl.when(gy != peer)
        def _(peer=peer):
            slab(peer).wait_send()
            pltpu.make_async_remote_copy(
                src_ref=heat.at[:, :, pl.ds(0, tile_y)],
                dst_ref=tile.at[pl.ds(peer * width, width)],
                send_sem=send_sem.at[peer],
                recv_sem=recv_sem.at[peer],
                device_id=(gx, peer),
                device_id_type=MESH,
            ).wait_recv()
    for level in range(base.shape[0]):
        out[level] = base[level] + tile[:, level, :]


def tn_dot(left, right):
    return lax.dot_general(
        left, right, (((0,), (0,)), ((), ())), preferred_element_type=jnp.float32
    )


def three_parts(rows):
    high = rows.astype(jnp.bfloat16).astype(jnp.float32)
    rest = rows - high
    middle = rest.astype(jnp.bfloat16).astype(jnp.float32)
    return jnp.concatenate([high, middle, rest - middle], axis=0).astype(jnp.bfloat16)


def chem_kernel(levels, width, edge, *refs):
    if edge:
        (flags, rim, halo_w, halo_e, tracer, strip, sun, bins, kinds, table, settle, light,
         _out_in, _opt_in, out, opt, first, second, zonal, merid, rounded) = refs
    else:
        (tracer, strip, sun, bins, kinds, table, settle, light,
         out, opt, first, second, zonal, merid, rounded) = refs
    level = levels - 1 - pl.program_id(0)
    step = pl.program_id(1)
    ny = tracer.shape[2]
    fields = strip.shape[1]
    local = first.shape[0]
    chunk = 64

    def selector(row):
        which = lax.rem(lax.broadcasted_iota(jnp.int32, (3 * fields, 128), 0), fields)
        return jnp.where(which == row, 1.0, 0.0).astype(jnp.bfloat16)

    def coefficients(slot, rows):
        parts = three_parts(rows)
        zonal[slot] = tn_dot(parts, selector(level))
        merid[slot] = tn_dot(parts, selector(levels + level))

    def moved(source, slot, y):
        here = source[slot, pl.ds(PAD + y, chunk), :]
        c = zonal[slot, pl.ds(y, chunk), :]
        d = merid[slot, pl.ds(y, chunk), :]
        across = jnp.where(
            c > 0.0,
            source[slot - 1, pl.ds(PAD + y, chunk), :],
            source[slot + 1, pl.ds(PAD + y, chunk), :],
        )
        along = jnp.where(
            d > 0.0,
            source[slot, pl.ds(PAD - 1 + y, chunk), :],
            source[slot, pl.ds(PAD + 1 + y, chunk), :],
        )
        return here + jnp.abs(c) * (across - here) + jnp.abs(d) * (along - here)

    def advance(source, target, low, high):
        def column(slot, carry):
            for y in range(0, ny, chunk):
                target[slot, pl.ds(PAD + y, chunk), :] = moved(source, slot, y)
            return carry

        lax.fori_loop(low, high, column, 0)

    def prepare():
        advance(first, second, 1, local - 1)
        advance(second, first, 2, local - 2)

    @pl.when((pl.program_id(0) == 0) & (step == 0))
    def _():
        zeros = jnp.zeros((local, PAD, 128), jnp.float32)
        for buffer in (first, second):
            buffer[:, pl.ds(0, PAD), :] = zeros
            buffer[:, pl.ds(PAD + ny, PAD), :] = zeros

    body = pl.ds(PAD, ny)
    if edge:
        six = local - SUB

        @pl.when(step == 0)
        def _():
            for j in range(SUB):
                rows = jnp.where(flags[0] == 1, rim[0, j], strip[j])
                coefficients(j, jnp.where(flags[1] == 1, rows, 0.0))
                first[j, body, :] = halo_w[0, j].astype(jnp.float32)

            def load(j, carry):
                coefficients(j + SUB, strip[j + SUB])
                first[j + SUB, body, :] = tracer[0, j].astype(jnp.float32)
                return carry

            lax.fori_loop(0, six, load, 0)
            prepare()

        @pl.when(step == SUB)
        def _():
            def load(j, carry):
                coefficients(j, strip[width - SUB + j])
                first[j, body, :] = tracer[0, width - six + j].astype(jnp.float32)
                return carry

            lax.fori_loop(0, six, load, 0)
            for j in range(SUB):
                rows = jnp.where(flags[2] == 1, rim[1, j], strip[width + SUB + j])
                coefficients(six + j, jnp.where(flags[3] == 1, rows, 0.0))
                first[six + j, body, :] = halo_e[0, j].astype(jnp.float32)
            prepare()

        slot = SUB + lax.rem(step, SUB)
        column = jnp.where(step < SUB, step, step + width - 2 * SUB)
    else:
        @pl.when(step == 0)
        def _():
            def load(j, carry):
                coefficients(j, strip[j + SUB])
                first[j, body, :] = tracer[0, j].astype(jnp.float32)
                return carry

            lax.fori_loop(0, local, load, 0)
            prepare()

        slot = SUB + step
        column = slot

    kind_row = kinds[pl.ds(column, 1), :]
    rows_here = strip[column + SUB]

    @pl.when(level == 0)
    def _():
        which = lax.rem(lax.broadcasted_iota(jnp.int32, (3 * LAND_ROWS, ny), 0), LAND_ROWS)
        one_hot = jnp.where(which == kind_row, 1.0, 0.0).astype(jnp.bfloat16)
        speed = tn_dot(one_hot, settle[...])
        depth = tn_dot(three_parts(rows_here), selector(3 * levels))
        second[0, body, :] = depth / (depth + speed)

    @pl.when(level == 0)
    def _():
        for y in range(0, ny, chunk):
            now = moved(first, slot, y) * second[0, pl.ds(PAD + y, chunk), :]
            out[0, 0, pl.ds(y, chunk), :] = now
            rounded[pl.ds(y, chunk), :] = now.astype(jnp.bfloat16)

    @pl.when(level != 0)
    def _():
        for y in range(0, ny, chunk):
            now = moved(first, slot, y)
            out[0, 0, pl.ds(y, chunk), :] = now
            rounded[pl.ds(y, chunk), :] = now.astype(jnp.bfloat16)

    projected = lax.dot_general(
        table[...], rounded[...], (((1,), (1,)), ((), ())), preferred_element_type=jnp.float32
    )
    bin_row = bins[pl.ds(column, 1), :]
    half = NBIN * 2 * NW
    dry = jnp.zeros((2 * NW, ny), jnp.float32)
    wet = jnp.zeros((2 * NW, ny), jnp.float32)
    for k in range(NBIN):
        chosen = bin_row == k
        dry = dry + jnp.where(chosen, projected[2 * NW * k : 2 * NW * (k + 1)], 0.0)
        wet = wet + jnp.where(chosen, projected[half + 2 * NW * k : half + 2 * NW * (k + 1)], 0.0)
    moisture = strip[column + SUB, pl.ds(2 * levels + level, 1), :]
    thickness = strip[column + SUB, pl.ds(3 * levels + level, 1), :]
    growth = moisture / (1.0 - moisture)
    opt[0, 0] = (dry + growth * wet) * thickness


def chem_call(edge, extras, shared, earlier):
    tracer, strip, sun, bins, kinds, table, settle, light = shared
    levels, width, ny, species = tracer.shape
    local = 3 * SUB if edge else width
    steps = 2 * SUB if edge else width - 2 * SUB
    last = levels - 1

    if edge:
        def place(l, i):
            return (last - l, jnp.where(i < SUB, i, i + width - 2 * SUB), 0, 0)
    else:
        def place(l, i):
            return (last - l, i + SUB, 0, 0)

    def whole(l, i):
        return (last - l, 0, 0, 0)

    halo_spec = pl.BlockSpec((1, SUB, ny, species), whole)
    in_specs = [pl.BlockSpec((1, width, ny, species), whole)] + [VMEM_SPEC] * 6 + [SMEM_SPEC]
    aliases = {}
    if edge:
        in_specs = [SMEM_SPEC, VMEM_SPEC, halo_spec, halo_spec] + in_specs
        in_specs += [pl.BlockSpec(memory_space=pl.ANY)] * 2
        aliases = {len(in_specs) - 2: 0, len(in_specs) - 1: 1}
    cells = levels * local * ny * species
    return pl.pallas_call(
        functools.partial(chem_kernel, levels, width, edge),
        grid=(levels, steps),
        in_specs=in_specs,
        out_specs=[
            pl.BlockSpec((1, 1, ny, species), place),
            pl.BlockSpec((1, 1, 2 * NW, ny), place),
        ],
        out_shape=[
            jax.ShapeDtypeStruct((levels, width, ny, species), jnp.float32),
            jax.ShapeDtypeStruct((levels, width, 2 * NW, ny), jnp.float32),
        ],
        scratch_shapes=[
            pltpu.VMEM((local, ny + 2 * PAD, species), jnp.float32),
            pltpu.VMEM((local, ny + 2 * PAD, species), jnp.float32),
            pltpu.VMEM((local, ny, species), jnp.float32),
            pltpu.VMEM((local, ny, species), jnp.float32),
            pltpu.VMEM((ny, species), jnp.bfloat16),
        ],
        input_output_aliases=aliases,
        compiler_params=pltpu.CompilerParams(
            dimension_semantics=("arbitrary", "arbitrary"),
            vmem_limit_bytes=60 * 1024 * 1024,
        ),
        cost_estimate=pl.CostEstimate(
            flops=cells * 40, bytes_accessed=cells * 6, transcendentals=0
        ),
        name="edge_columns" if edge else "inner_columns",
    )(*extras, tracer, strip, sun, bins, kinds, table, settle, light, *earlier)


def radiate(optical, cosine, sunlight):
    overhead = jnp.zeros_like(optical[0, :, :NW])
    layers = [None] * optical.shape[0]
    for height in reversed(range(optical.shape[0])):
        transmitted = jnp.exp(-overhead / cosine[:, None])
        layers[height] = cosine * jnp.sum(
            sunlight[None, :, None] * optical[height, :, NW:] * transmitted, axis=1
        )
        overhead = overhead + optical[height, :, :NW]
    return jnp.stack(layers, axis=1)


def per_device(
    tracer_amounts,
    zonal_transit_ratio,
    meridional_transit_ratio,
    moisture_ratio,
    stratum_depths,
    sun_elevation_factor,
    thermal_anomaly,
    particle_class_map,
    ground_cover_kind,
    arid_extinction_table,
    swelling_factors,
    settling_velocities,
    arriving_irradiance,
):
    levels, width, ny, species = tracer_amounts.shape
    gx_count = lax.axis_size("gx")
    gy_count = lax.axis_size("gy")
    total = gx_count * gy_count
    gx = lax.axis_index("gx")
    gy = lax.axis_index("gy")
    tile_x, tile_y = sun_elevation_factor.shape
    both = ("gx", "gy")
    halo_w = lax.ppermute(
        tracer_amounts[:, width - SUB :], both, [(i, i + 1) for i in range(total - 1)]
    )
    halo_e = lax.ppermute(
        tracer_amounts[:, :SUB], both, [(i + 1, i) for i in range(total - 1)]
    )

    fields = jnp.concatenate(
        [zonal_transit_ratio, meridional_transit_ratio, moisture_ratio, stratum_depths], axis=0
    )
    field_count = fields.shape[0]
    fields = jnp.pad(fields.transpose(1, 0, 2), ((SUB, SUB), (0, 0), (0, 0)))
    t = thermal_anomaly
    span_y = max(tile_x, tile_y)

    def edge_rows(rows):
        return jnp.pad(rows, ((0, 8 - levels), (0, span_y - rows.shape[1])))

    fringe = jnp.stack(
        [edge_rows(t[:, 0]), edge_rows(t[:, -1]), edge_rows(t[:, :, 0]), edge_rows(t[:, :, -1])]
    )
    dma = pltpu.SemaphoreType.DMA
    strip, rim, strip_sun, fringe_in = pl.pallas_call(
        functools.partial(fields_kernel, gx_count, gy_count, width),
        in_specs=[VMEM_SPEC] * 3,
        out_specs=[VMEM_SPEC] * 4,
        out_shape=[
            jax.ShapeDtypeStruct((width + 2 * SUB, field_count, ny), jnp.float32),
            jax.ShapeDtypeStruct((2, SUB, field_count, ny), jnp.float32),
            jax.ShapeDtypeStruct((width, ny), jnp.float32),
            jax.ShapeDtypeStruct(fringe.shape, jnp.float32),
        ],
        scratch_shapes=[
            dma((gy_count,)), dma((gy_count,)), dma((gy_count,)), dma((gy_count,)),
            dma((2,)), dma((gy_count,)), dma((4,)), dma((4,)),
        ],
        compiler_params=pltpu.CompilerParams(collective_id=0, has_side_effects=True),
        name="field_exchange",
    )(fields, sun_elevation_factor, fringe)

    east_row = jnp.where(gx == gx_count - 1, 0.0, fringe_in[0, :levels, :tile_y])
    west_row = jnp.where(gx == 0, 0.0, fringe_in[1, :levels, :tile_y])
    north_col = jnp.where(gy == gy_count - 1, 0.0, fringe_in[2, :levels, :tile_x])
    south_col = jnp.where(gy == 0, 0.0, fringe_in[3, :levels, :tile_x])
    wide_x = jnp.concatenate([west_row[:, None], t, east_row[:, None]], axis=1)
    wide_y = jnp.concatenate([south_col[:, :, None], t, north_col[:, :, None]], axis=2)
    laplace = wide_x[:, 2:] + wide_x[:, :-2] + wide_y[:, :, 2:] + wide_y[:, :, :-2] - 4.0 * t
    base = t + SPREAD_FACTOR * laplace

    table = jnp.concatenate([arid_extinction_table, swelling_factors], axis=1).T
    land = jnp.pad(
        settling_velocities, ((0, LAND_ROWS - settling_velocities.shape[0]), (0, 0))
    )
    high = lax.reduce_precision(land, 8, 7)
    middle = lax.reduce_precision(land - high, 8, 7)
    settle = jnp.concatenate([high, middle, land - high - middle], axis=0).astype(jnp.bfloat16)
    shared = (
        tracer_amounts, strip, strip_sun, particle_class_map, ground_cover_kind,
        table, settle, arriving_irradiance,
    )
    updated, optical = chem_call(False, (), shared, ())
    flags = jnp.stack(
        [gy == 0, (gx > 0) | (gy > 0), gy == gy_count - 1, (gx < gx_count - 1) | (gy < gy_count - 1)]
    ).astype(jnp.int32)
    updated, optical = chem_call(
        True, (flags, rim, halo_w, halo_e), shared, (updated, optical)
    )
    heat = radiate(optical, strip_sun, arriving_irradiance)
    anomaly = pl.pallas_call(
        functools.partial(return_kernel, gx_count, gy_count, width),
        in_specs=[VMEM_SPEC] * 2,
        out_specs=VMEM_SPEC,
        out_shape=jax.ShapeDtypeStruct(t.shape, jnp.float32),
        scratch_shapes=[
            pltpu.VMEM((tile_x, levels, tile_y), jnp.float32),
            dma((gy_count,)), dma((gy_count,)),
        ],
        compiler_params=pltpu.CompilerParams(collective_id=1, has_side_effects=True),
        name="heat_return",
    )(heat, base)
    return (updated, anomaly)


def solution(mesh):
    return jax.shard_map(
        per_device,
        mesh=mesh,
        in_specs=(
            P(None, ("gx", "gy"), None, None),
            P(None, "gx", "gy"),
            P(None, "gx", "gy"),
            P(None, "gx", "gy"),
            P(None, "gx", "gy"),
            P("gx", "gy"),
            P(None, "gx", "gy"),
            P(("gx", "gy"), None),
            P(("gx", "gy"), None),
            P(),
            P(),
            P(),
            P(),
        ),
        out_specs=(P(None, ("gx", "gy"), None, None), P(None, "gx", "gy")),
        check_vma=False,
    )
```

time: 169 us -> 129 us (0.76)
  Pallas kernels: 0 us -> 98 us
  other arithmetic: 56.4 us -> 9.04 us
  local copies, waits for them, and re-layouts: 42.3 us -> 10.5 us
  starting transfers between devices: 38.4 us -> 9.16 us
  waiting for transfers between devices: 21.4 us -> 0.01 us
  matrix products: 7.92 us -> 0 us
    pallas_call x0 -> x4, Pallas kernels: none -> 98 us  [the longest x2 56 us: chem_call(): pl.pallas_call(functools.partial(chem_kernel, levels, width, edge), grid=...]
    mul x4 -> x1, other arithmetic: 39.6 us -> 0.01 us  [radiate(): cosine * jnp.sum(sunlight[None, :, None] * optical[height, :, NW:] * tran...]
    ppermute x8 -> x2, waiting for transfers between devices: 21.3 us -> 0.01 us  [the longest x1 0.01 us: per_device(): lax.ppermute(tracer_amounts[:, width - SUB:], both, [(i, i + 1) for i in...]
    ppermute x8 -> x2, starting transfers between devices: 30.1 us -> 9.16 us  [the longest x1 5.67 us: per_device(): lax.ppermute(tracer_amounts[:, :SUB], both, [(i + 1, i) for i in range(to...]
    unnamed x39 -> x15, local copies, waits for them, and re-layouts: 17.5 us -> 6.2 us
    slice x17 -> x3, local copies, waits for them, and re-layouts: 13.2 us -> 3.31 us  [the longest x1 1.51 us: per_device(): tracer_amounts[:, :SUB]]
    all_to_all x2 -> x0, starting transfers between devices: 8.34 us -> none  [the longest x1 4.87 us: per_device(): lax.all_to_all(fields, 'gy', split_axis=1, concat_axis=2, tiled=True)]
    dot_general x2 -> x0, matrix products: 7.92 us -> none  [the longest x1 6.66 us: per_device(): jnp.dot(one_hot.reshape(-1, land_count), settling_velocities, precision=l...]
  transfers between devices with their start and end apart: 10 -> 2, of which waited for: 4 -> 0; matrix products, arithmetic and copies ran while one was open for 8% -> 10% of each run, Pallas kernels for 0% -> 51%
where the time goes in v1:
time: 129 us; the launch traced here: 128 us
  Pallas kernels  98 us (76%)
  local copies, waits for them, and re-layouts  10.5 us (8%)
  starting transfers between devices  9.16 us (7%)
  other arithmetic  9.04 us (7%)
    pallas_call x2, Pallas kernels, chem_call(): pl.pallas_call(functools.partial(chem_kernel, levels, width, edge), grid=...  56 us
    pallas_call x1, Pallas kernels, per_device(): pl.pallas_call(functools.partial(fields_kernel, gx_count, gy_count, width...  34.9 us
    pallas_call x1, Pallas kernels, per_device(): pl.pallas_call(functools.partial(return_kernel, gx_count, gy_count, width...  7.15 us
    unnamed x15, local copies, waits for them, and re-layouts  6.2 us
    ppermute x1, starting transfers between devices, per_device(): lax.ppermute(tracer_amounts[:, :SUB], both, [(i + 1, i) for i in range(to...  5.67 us
    ppermute x1, starting transfers between devices, per_device(): lax.ppermute(tracer_amounts[:, width - SUB:], both, [(i, i + 1) for i in...  3.48 us
  transfers between devices with their start and end apart: 2, of which 0 were waited for; matrix products, arithmetic and copies ran while one was open for 10% of the time, Pallas kernels for 51%

profile of v1, /device:TPU:4, one launch (start us, length us, event | category | flops | bytes accessed | tf_op | source)
XLA Modules:
  0.0 127.5 jit_solution(8354014293790763)
XLA Ops:
  0.6 0.0 copy-start.3
  0.6 1.5 %fusion.12 = (bf16[2,3,512,128]{3,2,1,0:T(8,128)(2,1)S(1)}, bf16[2,3,512,128]{3,2,1,0:T(8,128)(2,1)S(1)}) fusion(bf16[2,16,512,128]{3,2,1,0:T(8,128)(2,1)} %refs_4_.3), kind=kLoop, calls=%fused_computation.40 | loop fusion | bytes 3145728 | tf_op jit(solution)/shard_map/slice | solution.py:450
  2.2 3.5 %collective-permute-start = (bf16[2,3,512,128]{3,2,1,0:T(8,128)(2,1)S(1)}, bf16[2,3,512,128]{3,2,1,0:T(8,128)(2,1)S(1)}, u32[]{:S(2)}, u32[]{:S(2)}) collective-permute-start(bf16[2,3,512,128]{3,2,1,0:T(8,128)(2,1)S(1)} %get-tuple-element.23), channel_id=1, source_target_pairs={{0,1},{1,2},{2,3},{3,4},{4,5},{5,6},{6,7},{7,8},{8,9},{9,10},{10,1... | collective-permute-start | bytes 2359304 | tf_op jit(solution)/shard_map/ppermute | solution.py:446
  5.6 5.7 %collective-permute-start.1 = (bf16[2,3,512,128]{3,2,1,0:T(8,128)(2,1)S(1)}, bf16[2,3,512,128]{3,2,1,0:T(8,128)(2,1)S(1)}, u32[]{:S(2)}, u32[]{:S(2)}) collective-permute-start(bf16[2,3,512,128]{3,2,1,0:T(8,128)(2,1)S(1)} %get-tuple-element.22), channel_id=1, source_target_pairs={{1,0},{2,1},{3,2},{4,3},{5,4},{6,5},{7,6},{8,7},{9,8},{10,9},{11,1... | collective-permute-start | bytes 2359304 | tf_op jit(solution)/shard_map/ppermute | solution.py:449
  11.3 1.1 slice_reduce_fusion.1
  12.4 0.7 fusion.13
  13.1 0.9 copy.26
  14.0 0.9 copy.27
  14.9 0.9 copy.28
  15.8 0.9 copy.29
  16.7 0.7 reduce-precision_convert_fusion.1
  17.5 0.1 maximum_bitcast_fusion
  17.6 0.7 pad.22.fields
  18.3 0.6 pad_maximum_fusion.6.fringe
  18.9 34.9 %field_exchange.1 = (f32[22,8,512]{2,1,0:T(8,128)}, f32[2,3,8,512]{3,2,1,0:T(8,128)}, f32[16,512]{1,0:T(8,128)}, f32[4,8,128]{2,1,0:T(8,128)}) custom-call(f32[70,8,128]{2,1,0:T(8,128)} %pad.22.fields, f32[64,128]{1,0:T(8,128)} %sun.1, f32[4,8,128]{2,1,0:T(8,128)} %pad_maximum_fusion.6.fringe), custom_call_target="tpu_custom_call" | custom-call | tf_op jit(solution)/shard_map/field_exchange/pallas_call | solution.py:468
  53.8 0.7 select_bitcast_fusion.1
  54.5 0.1 copy.33
  54.6 0.1 copy.34
  54.7 1.4 %maximum_bitcast_fusion.1.refs_5_.refs_9_ = bf16[128,128]{1,0:T(8,128)(2,1)} fusion(bf16[128,64]{0,1:T(8,128)(2,1)} %param.23, bf16[128,64]{0,1:T(8,128)(2,1)} %param.22), kind=kLoop, calls=%fused_computation.22 | loop fusion | flops 65536 | bytes 65536 | tf_op jit(solution)/shard_map/transpose | solution.py:495
  56.1 0.6 pad_maximum_fusion.5.refs_6_.refs_10_
  56.7 30.3 %inner_columns.1 = (f32[2,16,512,128]{3,2,1,0:T(8,128)}, f32[2,16,8,512]{3,2,1,0:T(8,128)}) custom-call(bf16[2,16,512,128]{3,2,1,0:T(8,128)(2,1)} %refs_4_.3, f32[22,8,512]{2,1,0:T(8,128)} %get-tuple-element.11.refs_1_.refs_5_, f32[16,512]{1,0:T(8,128)} %get-tuple-element.12.refs_2_.refs_6_, s32[16,512]{1,0:T(8,128)} %refs_7_.3, s32[16,512]{1,0:T(8,128)} %refs_8_.1, ...), custom_call_target="tpu_custom_call" | custom-call | flops 83886080 | bytes 12582912 | tf_op jit(solution)/shard_map/inner_columns/pallas_call | solution.py:380
  87.0 0.0 copy-start
  87.0 0.0 copy-start.4
  87.0 0.6 add_convert_fusion.refs_0_
  87.6 0.7 slice_select_fusion.1
  88.3 0.8 divide_exponential_fusion
  89.1 0.0 copy-done.3
  89.1 0.8 fusion.8.base
  89.8 0.0 collective-permute-done.refs_2_
  89.8 0.0 copy-start.1
  89.8 0.0 collective-permute-done.1.refs_3_
  89.9 0.0 copy-start.2
  89.9 0.9 copy-done.1
  90.7 0.3 copy-done.2
  91.0 25.7 %edge_columns.1 = (f32[2,16,512,128]{3,2,1,0:T(8,128)}, f32[2,16,8,512]{3,2,1,0:T(8,128)}) custom-call(s32[4]{0:T(128)} %add_convert_fusion.refs_0_, f32[2,3,8,512]{3,2,1,0:T(8,128)} %get-tuple-element.10.refs_1_, bf16[2,3,512,128]{3,2,1,0:T(8,128)(2,1)} %copy-done.1, ...), custom_call_target="tpu_custom_call", output_to_operand_aliasing={{0}: (12, {}), {1}: (13, {})} | custom-call | flops 47185920 | bytes 7077888 | tf_op jit(solution)/shard_map/edge_columns/pallas_call | solution.py:380
  116.7 0.0 copy-done
  116.7 0.0 copy-done.4
  116.7 1.4 %fusion.4 = (f32[16,512]{1,0:T(8,128)S(1)}, f32[16,512]{1,0:T(8,128)S(1)}) fusion(f32[2,16,8,512]{3,2,1,0:T(8,128)} %get-tuple-element.16, f32[16,512]{1,0:T(8,128)S(1)} %copy-done, f32[4]{0:T(128)S(1)} %copy-done.4, f32[16,512]{1,0:T(8,128)S(1)} %divide_exponential_fusion), kind=kLoop, calls=%fused_computation.8 | loop fusion | flops 245760 | bytes 524304 | tf_op jit(solution)/shard_map/reduce_sum | solution.py:416
  118.2 0.7 pad_maximum_fusion.4.heat
  118.9 7.2 %heat_return.1 = f32[2,64,128]{2,1,0:T(8,128)} custom-call(f32[16,2,512]{2,1,0:T(2,128)} %pad_maximum_fusion.4.heat, f32[2,64,128]{2,1,0:T(8,128)} %fusion.8.base), custom_call_target="tpu_custom_call" | custom-call | tf_op jit(solution)/shard_map/heat_return/pallas_call | solution.py:514
  126.1 1.5 %copy.40 = f32[2,64,128]{2,1,0:T(8,128)} copy(f32[2,64,128]{2,1,0:T(8,128)} %heat_return.1) | data formatting | bytes 131072
  (5 shorter events, 0.1 us)
Async XLA Ops:
  0.6 88.5 %copy-start.3 = (f32[2,64,128]{2,1,0:T(8,128)S(1)}, f32[2,64,128]{2,1,0:T(8,128)}, u32[]{:S(2)}) copy-start(f32[2,64,128]{2,1,0:T(8,128)} %param.19) | copy-start | bytes 196612
  2.2 87.7 %collective-permute-start = (bf16[2,3,512,128]{3,2,1,0:T(8,128)(2,1)S(1)}, bf16[2,3,512,128]{3,2,1,0:T(8,128)(2,1)S(1)}, u32[]{:S(2)}, u32[]{:S(2)}) collective-permute-start(bf16[2,3,512,128]{3,2,1,0:T(8,128)(2,1)S(1)} %get-tuple-element.23), channel_id=1, source_target_pairs={{0,1},{1,2},{2,3},{3,4},{4,5},{5,6},{6,7},{7,8},{8,9},{9,10},{10,1... | collective-permute-start | bytes 2359304 | tf_op jit(solution)/shard_map/ppermute | solution.py:446
  5.6 84.2 %collective-permute-start.1 = (bf16[2,3,512,128]{3,2,1,0:T(8,128)(2,1)S(1)}, bf16[2,3,512,128]{3,2,1,0:T(8,128)(2,1)S(1)}, u32[]{:S(2)}, u32[]{:S(2)}) collective-permute-start(bf16[2,3,512,128]{3,2,1,0:T(8,128)(2,1)S(1)} %get-tuple-element.22), channel_id=1, source_target_pairs={{1,0},{2,1},{3,2},{4,3},{5,4},{6,5},{7,6},{8,7},{9,8},{10,9},{11,1... | collective-permute-start | bytes 2359304 | tf_op jit(solution)/shard_map/ppermute | solution.py:449
  87.0 29.7 %copy-start = (f32[16,512]{1,0:T(8,128)S(1)}, f32[16,512]{1,0:T(8,128)}, u32[]{:S(2)}) copy-start(f32[16,512]{1,0:T(8,128)} %get-tuple-element.12.refs_2_.refs_6_) | copy-start | bytes 98308
  87.0 29.7 %copy-start.4 = (f32[4]{0:T(128)S(1)}, f32[4]{0:T(128)}, u32[]{:S(2)}) copy-start(f32[4]{0:T(128)} %refs_11_.1) | copy-start | bytes 52
  89.8 0.9 copy-start.1
  89.9 1.1 copy-start.2

commit v2 on v1

--- a/solution.py
+++ b/solution.py
@@ -443,13 +443,6 @@
     gy = lax.axis_index("gy")
     tile_x, tile_y = sun_elevation_factor.shape
     both = ("gx", "gy")
-    halo_w = lax.ppermute(
-        tracer_amounts[:, width - SUB :], both, [(i, i + 1) for i in range(total - 1)]
-    )
-    halo_e = lax.ppermute(
-        tracer_amounts[:, :SUB], both, [(i + 1, i) for i in range(total - 1)]
-    )
-
     fields = jnp.concatenate(
         [zonal_transit_ratio, meridional_transit_ratio, moisture_ratio, stratum_depths], axis=0
     )
@@ -482,6 +475,12 @@
         compiler_params=pltpu.CompilerParams(collective_id=0, has_side_effects=True),
         name="field_exchange",
     )(fields, sun_elevation_factor, fringe)
+
+    tail, head, strip = lax.optimization_barrier(
+        (tracer_amounts[:, width - SUB :], tracer_amounts[:, :SUB], strip)
+    )
+    halo_w = lax.ppermute(tail, both, [(i, i + 1) for i in range(total - 1)])
+    halo_e = lax.ppermute(head, both, [(i + 1, i) for i in range(total - 1)])
 
     east_row = jnp.where(gx == gx_count - 1, 0.0, fringe_in[0, :levels, :tile_y])
     west_row = jnp.where(gx == 0, 0.0, fringe_in[1, :levels, :tile_y])

time: 129 us -> 111 us (0.86)
  Pallas kernels: 98 us -> 80.8 us
    pallas_call x1, Pallas kernels: 34.9 us -> 17.6 us  [per_device(): pl.pallas_call(functools.partial(fields_kernel, gx_count, gy_count, width...]
  transfers between devices with their start and end apart: 2 -> 2, of which waited for: 0 -> 0; matrix products, arithmetic and copies ran while one was open for 10% -> 6% of each run, Pallas kernels for 51% -> 27%
where the time goes in v2:
time: 111 us; the launch traced here: 110 us
  Pallas kernels  80.8 us (73%)
  local copies, waits for them, and re-layouts  10.5 us (9%)
  starting transfers between devices  9.16 us (8%)
  other arithmetic  9.04 us (8%)
    pallas_call x2, Pallas kernels, chem_call(): pl.pallas_call(functools.partial(chem_kernel, levels, width, edge), grid=...  56 us
    pallas_call x1, Pallas kernels, per_device(): pl.pallas_call(functools.partial(fields_kernel, gx_count, gy_count, width...  17.6 us
    pallas_call x1, Pallas kernels, per_device(): pl.pallas_call(functools.partial(return_kernel, gx_count, gy_count, width...  7.15 us
    ppermute x1, starting transfers between devices, per_device(): halo_e = lax.ppermute(head, both, [(i + 1, i) for i in range(total - 1)])  7.02 us
    unnamed x15, local copies, waits for them, and re-layouts  6.2 us
  transfers between devices with their start and end apart: 2, of which 0 were waited for; matrix products, arithmetic and copies ran while one was open for 6% of the time, Pallas kernels for 27%

profile of v2, /device:TPU:4, one launch (start us, length us, event | category | flops | bytes accessed | tf_op | source)
XLA Modules:
  0.0 110.3 jit_solution(4739384671035663645)
XLA Ops:
  0.6 0.0 copy-start.3
  0.6 1.1 slice_reduce_fusion.1
  1.7 0.7 fusion.13
  2.5 0.9 copy.26
  3.4 0.9 copy.27
  4.3 0.9 copy.28
  5.2 0.9 copy.29
  6.1 1.5 %fusion.12 = (bf16[2,3,512,128]{3,2,1,0:T(8,128)(2,1)S(1)}, bf16[2,3,512,128]{3,2,1,0:T(8,128)(2,1)S(1)}) fusion(bf16[2,16,512,128]{3,2,1,0:T(8,128)(2,1)} %refs_4_.3), kind=kLoop, calls=%fused_computation.40 | loop fusion | bytes 3145728 | tf_op jit(solution)/shard_map/slice | solution.py:480
  7.6 0.1 maximum_bitcast_fusion
  7.7 0.7 pad.22.fields
  8.4 0.6 pad_maximum_fusion.6.fringe
  9.0 17.6 %field_exchange.1 = (f32[22,8,512]{2,1,0:T(8,128)}, f32[2,3,8,512]{3,2,1,0:T(8,128)}, f32[16,512]{1,0:T(8,128)}, f32[4,8,128]{2,1,0:T(8,128)}) custom-call(f32[70,8,128]{2,1,0:T(8,128)} %pad.22.fields, f32[64,128]{1,0:T(8,128)} %sun.1, f32[4,8,128]{2,1,0:T(8,128)} %pad_maximum_fusion.6.fringe), custom_call_target="tpu_custom_call" | custom-call | tf_op jit(solution)/shard_map/field_exchange/pallas_call | solution.py:461
  26.7 2.1 %collective-permute-start = (bf16[2,3,512,128]{3,2,1,0:T(8,128)(2,1)S(1)}, bf16[2,3,512,128]{3,2,1,0:T(8,128)(2,1)S(1)}, u32[]{:S(2)}, u32[]{:S(2)}) collective-permute-start(bf16[2,3,512,128]{3,2,1,0:T(8,128)(2,1)S(1)} %get-tuple-element.15), channel_id=1, source_target_pairs={{0,1},{1,2},{2,3},{3,4},{4,5},{5,6},{6,7},{7,8},{8,9},{9,10},{10,1... | collective-permute-start | bytes 2359304 | tf_op jit(solution)/shard_map/ppermute | solution.py:482
  28.8 7.0 %collective-permute-start.1 = (bf16[2,3,512,128]{3,2,1,0:T(8,128)(2,1)S(1)}, bf16[2,3,512,128]{3,2,1,0:T(8,128)(2,1)S(1)}, u32[]{:S(2)}, u32[]{:S(2)}) collective-permute-start(bf16[2,3,512,128]{3,2,1,0:T(8,128)(2,1)S(1)} %get-tuple-element.16), channel_id=1, source_target_pairs={{1,0},{2,1},{3,2},{4,3},{5,4},{6,5},{7,6},{8,7},{9,8},{10,9},{11,1... | collective-permute-start | bytes 2359304 | tf_op jit(solution)/shard_map/ppermute | solution.py:483
  35.9 0.7 reduce-precision_convert_fusion.1
  36.6 0.7 select_bitcast_fusion.1
  37.3 0.1 copy.33
  37.4 0.1 copy.34
  37.5 1.4 %maximum_bitcast_fusion.1.refs_5_.refs_9_ = bf16[128,128]{1,0:T(8,128)(2,1)} fusion(bf16[128,64]{0,1:T(8,128)(2,1)} %param.23, bf16[128,64]{0,1:T(8,128)(2,1)} %param.22), kind=kLoop, calls=%fused_computation.22 | loop fusion | flops 65536 | bytes 65536 | tf_op jit(solution)/shard_map/transpose | solution.py:494
  38.9 0.6 pad_maximum_fusion.5.refs_6_.refs_10_
  39.5 30.3 %inner_columns.1 = (f32[2,16,512,128]{3,2,1,0:T(8,128)}, f32[2,16,8,512]{3,2,1,0:T(8,128)}) custom-call(bf16[2,16,512,128]{3,2,1,0:T(8,128)(2,1)} %refs_4_.3, f32[22,8,512]{2,1,0:T(8,128)} %get-tuple-element.17.refs_1_.refs_5_, f32[16,512]{1,0:T(8,128)} %get-tuple-element.18.refs_2_.refs_6_, s32[16,512]{1,0:T(8,128)} %refs_7_.3, s32[16,512]{1,0:T(8,128)} %refs_8_.1, ...), custom_call_target="tpu_custom_call" | custom-call | flops 83886080 | bytes 12582912 | tf_op jit(solution)/shard_map/inner_columns/pallas_call | solution.py:380
  69.8 0.0 copy-start
  69.8 0.0 copy-start.4
  69.8 0.6 add_convert_fusion.refs_0_
  70.3 0.7 slice_select_fusion.1
  71.0 0.8 divide_exponential_fusion
  71.8 0.0 copy-done.3
  71.8 0.8 fusion.8.base
  72.6 0.0 collective-permute-done.refs_2_
  72.6 0.0 copy-start.1
  72.6 0.0 collective-permute-done.1.refs_3_
  72.6 0.0 copy-start.2
  72.6 0.9 copy-done.1
  73.5 0.3 copy-done.2
  73.7 25.7 %edge_columns.1 = (f32[2,16,512,128]{3,2,1,0:T(8,128)}, f32[2,16,8,512]{3,2,1,0:T(8,128)}) custom-call(s32[4]{0:T(128)} %add_convert_fusion.refs_0_, f32[2,3,8,512]{3,2,1,0:T(8,128)} %get-tuple-element.13.refs_1_, bf16[2,3,512,128]{3,2,1,0:T(8,128)(2,1)} %copy-done.1, ...), custom_call_target="tpu_custom_call", output_to_operand_aliasing={{0}: (12, {}), {1}: (13, {})} | custom-call | flops 47185920 | bytes 7077888 | tf_op jit(solution)/shard_map/edge_columns/pallas_call | solution.py:380
  99.4 0.0 copy-done
  99.4 0.0 copy-done.4
  99.4 1.4 %fusion.4 = (f32[16,512]{1,0:T(8,128)S(1)}, f32[16,512]{1,0:T(8,128)S(1)}) fusion(f32[2,16,8,512]{3,2,1,0:T(8,128)} %get-tuple-element.22, f32[16,512]{1,0:T(8,128)S(1)} %copy-done, f32[4]{0:T(128)S(1)} %copy-done.4, f32[16,512]{1,0:T(8,128)S(1)} %divide_exponential_fusion), kind=kLoop, calls=%fused_computation.8 | loop fusion | flops 245760 | bytes 524304 | tf_op jit(solution)/shard_map/reduce_sum | solution.py:416
  100.9 0.7 pad_maximum_fusion.4.heat
  101.6 7.2 %heat_return.1 = f32[2,64,128]{2,1,0:T(8,128)} custom-call(f32[16,2,512]{2,1,0:T(2,128)} %pad_maximum_fusion.4.heat, f32[2,64,128]{2,1,0:T(8,128)} %fusion.8.base), custom_call_target="tpu_custom_call" | custom-call | tf_op jit(solution)/shard_map/heat_return/pallas_call | solution.py:513
  108.8 1.5 %copy.40 = f32[2,64,128]{2,1,0:T(8,128)} copy(f32[2,64,128]{2,1,0:T(8,128)} %heat_return.1) | data formatting | bytes 131072
  (5 shorter events, 0.1 us)
Async XLA Ops:
  0.6 71.2 %copy-start.3 = (f32[2,64,128]{2,1,0:T(8,128)S(1)}, f32[2,64,128]{2,1,0:T(8,128)}, u32[]{:S(2)}) copy-start(f32[2,64,128]{2,1,0:T(8,128)} %param.19) | copy-start | bytes 196612
  26.7 45.9 %collective-permute-start = (bf16[2,3,512,128]{3,2,1,0:T(8,128)(2,1)S(1)}, bf16[2,3,512,128]{3,2,1,0:T(8,128)(2,1)S(1)}, u32[]{:S(2)}, u32[]{:S(2)}) collective-permute-start(bf16[2,3,512,128]{3,2,1,0:T(8,128)(2,1)S(1)} %get-tuple-element.15), channel_id=1, source_target_pairs={{0,1},{1,2},{2,3},{3,4},{4,5},{5,6},{6,7},{7,8},{8,9},{9,10},{10,1... | collective-permute-start | bytes 2359304 | tf_op jit(solution)/shard_map/ppermute | solution.py:482
  28.8 43.8 %collective-permute-start.1 = (bf16[2,3,512,128]{3,2,1,0:T(8,128)(2,1)S(1)}, bf16[2,3,512,128]{3,2,1,0:T(8,128)(2,1)S(1)}, u32[]{:S(2)}, u32[]{:S(2)}) collective-permute-start(bf16[2,3,512,128]{3,2,1,0:T(8,128)(2,1)S(1)} %get-tuple-element.16), channel_id=1, source_target_pairs={{1,0},{2,1},{3,2},{4,3},{5,4},{6,5},{7,6},{8,7},{9,8},{10,9},{11,1... | collective-permute-start | bytes 2359304 | tf_op jit(solution)/shard_map/ppermute | solution.py:483
  69.8 29.7 %copy-start = (f32[16,512]{1,0:T(8,128)S(1)}, f32[16,512]{1,0:T(8,128)}, u32[]{:S(2)}) copy-start(f32[16,512]{1,0:T(8,128)} %get-tuple-element.18.refs_2_.refs_6_) | copy-start | bytes 98308
  69.8 29.7 %copy-start.4 = (f32[4]{0:T(128)S(1)}, f32[4]{0:T(128)}, u32[]{:S(2)}) copy-start(f32[4]{0:T(128)} %refs_11_.1) | copy-start | bytes 52
  72.6 0.9 copy-start.1
  72.6 1.1 %copy-start.2 = (bf16[2,3,512,128]{3,2,1,0:T(8,128)(2,1)}, bf16[2,3,512,128]{3,2,1,0:T(8,128)(2,1)S(1)}, u32[]{:S(2)}) copy-start(bf16[2,3,512,128]{3,2,1,0:T(8,128)(2,1)S(1)} %collective-permute-done.1.refs_3_) | copy-start | bytes 2359300

commit v3 on v2

--- a/solution.py
+++ b/solution.py
@@ -205,14 +205,14 @@
 
 def chem_kernel(levels, width, edge, *refs):
     if edge:
-        (flags, rim, halo_w, halo_e, tracer, strip, sun, bins, kinds, table, settle, light,
+        (flags, rim, halo_w, halo_e, saved, near_w, near_e, strip, bins, kinds, table, settle,
          _out_in, _opt_in, out, opt, first, second, zonal, merid, rounded) = refs
     else:
-        (tracer, strip, sun, bins, kinds, table, settle, light,
-         out, opt, first, second, zonal, merid, rounded) = refs
+        (tracer, strip, bins, kinds, table, settle,
+         out, opt, saved, first, second, zonal, merid, rounded) = refs
     level = levels - 1 - pl.program_id(0)
     step = pl.program_id(1)
-    ny = tracer.shape[2]
+    ny = strip.shape[2]
     fields = strip.shape[1]
     local = first.shape[0]
     chunk = 64
@@ -250,10 +250,6 @@
 
         lax.fori_loop(low, high, column, 0)
 
-    def prepare():
-        advance(first, second, 1, local - 1)
-        advance(second, first, 2, local - 2)
-
     @pl.when((pl.program_id(0) == 0) & (step == 0))
     def _():
         zeros = jnp.zeros((local, PAD, 128), jnp.float32)
@@ -263,38 +259,41 @@
 
     body = pl.ds(PAD, ny)
     if edge:
-        six = local - SUB
-
         @pl.when(step == 0)
         def _():
-            for j in range(SUB):
+            for j in (1, 2):
                 rows = jnp.where(flags[0] == 1, rim[0, j], strip[j])
                 coefficients(j, jnp.where(flags[1] == 1, rows, 0.0))
+            for j in (3, 4, 5):
+                coefficients(j, strip[j])
+            for j in range(SUB):
                 first[j, body, :] = halo_w[0, j].astype(jnp.float32)
-
-            def load(j, carry):
-                coefficients(j + SUB, strip[j + SUB])
-                first[j + SUB, body, :] = tracer[0, j].astype(jnp.float32)
-                return carry
-
-            lax.fori_loop(0, six, load, 0)
-            prepare()
+            for j in range(2):
+                first[SUB + j, body, :] = near_w[0, j].astype(jnp.float32)
+                second[SUB + 1 + j, body, :] = saved[0, j]
+            advance(first, second, 1, 4)
+            advance(second, first, 2, 5)
+            for j in range(2):
+                first[SUB + 2 + j, body, :] = saved[0, 2 + j]
 
         @pl.when(step == SUB)
         def _():
-            def load(j, carry):
-                coefficients(j, strip[width - SUB + j])
-                first[j, body, :] = tracer[0, width - six + j].astype(jnp.float32)
-                return carry
-
-            lax.fori_loop(0, six, load, 0)
+            for j in (1, 2, 3):
+                coefficients(j, strip[width - 1 + j])
+            for j in (4, 5):
+                rows = jnp.where(flags[2] == 1, rim[1, j - 4], strip[width - 1 + j])
+                coefficients(j, jnp.where(flags[3] == 1, rows, 0.0))
             for j in range(SUB):
-                rows = jnp.where(flags[2] == 1, rim[1, j], strip[width + SUB + j])
-                coefficients(six + j, jnp.where(flags[3] == 1, rows, 0.0))
-                first[six + j, body, :] = halo_e[0, j].astype(jnp.float32)
-            prepare()
-
-        slot = SUB + lax.rem(step, SUB)
+                first[4 + j, body, :] = halo_e[0, j].astype(jnp.float32)
+            for j in range(2):
+                first[2 + j, body, :] = near_e[0, j].astype(jnp.float32)
+                second[1 + j, body, :] = saved[0, 4 + j]
+            advance(first, second, 3, 6)
+            advance(second, first, 2, 5)
+            for j in range(2):
+                first[j, body, :] = saved[0, 6 + j]
+
+        slot = jnp.where(step < SUB, step + SUB, step - 2)
         column = jnp.where(step < SUB, step, step + width - 2 * SUB)
     else:
         @pl.when(step == 0)
@@ -305,7 +304,14 @@
                 return carry
 
             lax.fori_loop(0, local, load, 0)
-            prepare()
+            advance(first, second, 1, local - 1)
+            advance(second, first, 2, local - 2)
+            kept = (
+                (second, 1), (second, 2), (first, 2), (first, 3),
+                (second, local - 3), (second, local - 2), (first, local - 4), (first, local - 3),
+            )
+            for k, (buffer, place) in enumerate(kept):
+                saved[0, k] = buffer[place, body, :]
 
         slot = SUB + step
         column = slot
@@ -353,9 +359,9 @@
 
 
 def chem_call(edge, extras, shared, earlier):
-    tracer, strip, sun, bins, kinds, table, settle, light = shared
+    tracer, strip, bins, kinds, table, settle = shared
     levels, width, ny, species = tracer.shape
-    local = 3 * SUB if edge else width
+    local = 2 * SUB + 1 if edge else width
     steps = 2 * SUB if edge else width - 2 * SUB
     last = levels - 1
 
@@ -370,10 +376,19 @@
         return (last - l, 0, 0, 0)
 
     halo_spec = pl.BlockSpec((1, SUB, ny, species), whole)
-    in_specs = [pl.BlockSpec((1, width, ny, species), whole)] + [VMEM_SPEC] * 6 + [SMEM_SPEC]
+    kept_spec = pl.BlockSpec((1, 8, ny, species), whole)
+    in_specs = [pl.BlockSpec((1, width, ny, species), whole)] + [VMEM_SPEC] * 5
+    inputs = (tracer,)
     aliases = {}
     if edge:
-        in_specs = [SMEM_SPEC, VMEM_SPEC, halo_spec, halo_spec] + in_specs
+        far = width // 2 - 1
+        in_specs = [SMEM_SPEC, VMEM_SPEC, halo_spec, halo_spec, kept_spec]
+        in_specs += [
+            pl.BlockSpec((1, 2, ny, species), whole),
+            pl.BlockSpec((1, 2, ny, species), lambda l, i: (last - l, far, 0, 0)),
+        ]
+        in_specs += [VMEM_SPEC] * 5
+        inputs = (tracer, tracer)
         in_specs += [pl.BlockSpec(memory_space=pl.ANY)] * 2
         aliases = {len(in_specs) - 2: 0, len(in_specs) - 1: 1}
     cells = levels * local * ny * species
@@ -384,11 +399,13 @@
         out_specs=[
             pl.BlockSpec((1, 1, ny, species), place),
             pl.BlockSpec((1, 1, 2 * NW, ny), place),
-        ],
+        ]
+        + ([] if edge else [kept_spec]),
         out_shape=[
             jax.ShapeDtypeStruct((levels, width, ny, species), jnp.float32),
             jax.ShapeDtypeStruct((levels, width, 2 * NW, ny), jnp.float32),
-        ],
+        ]
+        + ([] if edge else [jax.ShapeDtypeStruct((levels, 8, ny, species), jnp.float32)]),
         scratch_shapes=[
             pltpu.VMEM((local, ny + 2 * PAD, species), jnp.float32),
             pltpu.VMEM((local, ny + 2 * PAD, species), jnp.float32),
@@ -405,7 +422,7 @@
             flops=cells * 40, bytes_accessed=cells * 6, transcendentals=0
         ),
         name="edge_columns" if edge else "inner_columns",
-    )(*extras, tracer, strip, sun, bins, kinds, table, settle, light, *earlier)
+    )(*extras, *inputs, strip, bins, kinds, table, settle, *earlier)
 
 
 def radiate(optical, cosine, sunlight):
@@ -499,15 +516,14 @@
     middle = lax.reduce_precision(land - high, 8, 7)
     settle = jnp.concatenate([high, middle, land - high - middle], axis=0).astype(jnp.bfloat16)
     shared = (
-        tracer_amounts, strip, strip_sun, particle_class_map, ground_cover_kind,
-        table, settle, arriving_irradiance,
-    )
-    updated, optical = chem_call(False, (), shared, ())
+        tracer_amounts, strip, particle_class_map, ground_cover_kind, table, settle,
+    )
+    updated, optical, saved = chem_call(False, (), shared, ())
     flags = jnp.stack(
         [gy == 0, (gx > 0) | (gy > 0), gy == gy_count - 1, (gx < gx_count - 1) | (gy < gy_count - 1)]
     ).astype(jnp.int32)
     updated, optical = chem_call(
-        True, (flags, rim, halo_w, halo_e), shared, (updated, optical)
+        True, (flags, rim, halo_w, halo_e, saved), shared, (updated, optical)
     )
     heat = radiate(optical, strip_sun, arriving_irradiance)
     anomaly = pl.pallas_call(

time: 111 us -> 102 us (0.919)
  Pallas kernels: 80.8 us -> 73.7 us
  other arithmetic: 9.04 us -> 6.87 us
    pallas_call x2, Pallas kernels: 56 us -> 48.9 us  [chem_call(): pl.pallas_call(functools.partial(chem_kernel, levels, width, edge), grid=...]
    unnamed x15 -> x21, local copies, waits for them, and re-layouts: 6.2 us -> 6.23 us
  transfers between devices with their start and end apart: 2 -> 2, of which waited for: 0 -> 0; matrix products, arithmetic and copies ran while one was open for 6% -> 4% of each run, Pallas kernels for 27% -> 31%
where the time goes in v3:
time: 102 us; the launch traced here: 101 us
  Pallas kernels  73.7 us (72%)
  local copies, waits for them, and re-layouts  10.5 us (10%)
  starting transfers between devices  9.16 us (9%)
  other arithmetic  6.87 us (7%)
    pallas_call x2, Pallas kernels, chem_call(): pl.pallas_call(functools.partial(chem_kernel, levels, width, edge), grid=...  48.9 us
    pallas_call x1, Pallas kernels, per_device(): pl.pallas_call(functools.partial(fields_kernel, gx_count, gy_count, width...  17.7 us
    pallas_call x1, Pallas kernels, per_device(): pl.pallas_call(functools.partial(return_kernel, gx_count, gy_count, width...  7.14 us
    ppermute x1, starting transfers between devices, per_device(): halo_e = lax.ppermute(head, both, [(i + 1, i) for i in range(total - 1)])  7.02 us
    unnamed x21, local copies, waits for them, and re-layouts  6.23 us
    ppermute x1, starting transfers between devices, per_device(): halo_w = lax.ppermute(tail, both, [(i, i + 1) for i in range(total - 1)])  2.14 us
  transfers between devices with their start and end apart: 2, of which 0 were waited for; matrix products, arithmetic and copies ran while one was open for 4% of the time, Pallas kernels for 31%

profile of v3, /device:TPU:4, one launch (start us, length us, event | category | flops | bytes accessed | tf_op | source)
XLA Modules:
  0.0 101.1 jit_solution(14590089983974983836)
XLA Ops:
  0.6 0.0 copy-start.6
  0.6 0.0 copy-start.5
  0.7 0.0 copy-start.4
  0.7 1.1 %slice_reduce_fusion.1 = (f32[2,64]{1,0:T(2,128)S(1)}, f32[2,64]{1,0:T(2,128)S(1)}) fusion(f32[2,64,128]{2,1,0:T(8,128)} %param.19), kind=kLoop, calls=%fused_computation.21 | loop fusion | bytes 2048 | tf_op jit(solution)/shard_map/slice | solution.py:475
  1.7 0.7 fusion.13
  2.5 0.9 copy.26
  3.4 0.9 copy.27
  4.3 0.9 copy.28
  5.2 0.9 copy.29
  6.1 0.0 copy-start.2
  6.1 1.5 %fusion.12 = (bf16[2,3,512,128]{3,2,1,0:T(8,128)(2,1)S(1)}, bf16[2,3,512,128]{3,2,1,0:T(8,128)(2,1)S(1)}) fusion(bf16[2,16,512,128]{3,2,1,0:T(8,128)(2,1)} %refs_6_.1), kind=kLoop, calls=%fused_computation.40 | loop fusion | bytes 3145728 | tf_op jit(solution)/shard_map/slice | solution.py:497
  7.6 0.1 maximum_bitcast_fusion
  7.7 0.7 pad.22.fields
  8.5 0.6 pad_maximum_fusion.6.fringe
  9.1 17.7 %field_exchange.1 = (f32[22,8,512]{2,1,0:T(8,128)}, f32[2,3,8,512]{3,2,1,0:T(8,128)}, f32[16,512]{1,0:T(8,128)}, f32[4,8,128]{2,1,0:T(8,128)}) custom-call(f32[70,8,128]{2,1,0:T(8,128)} %pad.22.fields, f32[64,128]{1,0:T(8,128)} %sun.1, f32[4,8,128]{2,1,0:T(8,128)} %pad_maximum_fusion.6.fringe), custom_call_target="tpu_custom_call" | custom-call | tf_op jit(solution)/shard_map/field_exchange/pallas_call | solution.py:478
  26.7 0.0 copy-start.3
  26.7 2.1 %collective-permute-start = (bf16[2,3,512,128]{3,2,1,0:T(8,128)(2,1)S(1)}, bf16[2,3,512,128]{3,2,1,0:T(8,128)(2,1)S(1)}, u32[]{:S(2)}, u32[]{:S(2)}) collective-permute-start(bf16[2,3,512,128]{3,2,1,0:T(8,128)(2,1)S(1)} %get-tuple-element.16), channel_id=1, source_target_pairs={{0,1},{1,2},{2,3},{3,4},{4,5},{5,6},{6,7},{7,8},{8,9},{9,10},{10,1... | collective-permute-start | bytes 2359304 | tf_op jit(solution)/shard_map/ppermute | solution.py:499
  28.9 7.0 %collective-permute-start.1 = (bf16[2,3,512,128]{3,2,1,0:T(8,128)(2,1)S(1)}, bf16[2,3,512,128]{3,2,1,0:T(8,128)(2,1)S(1)}, u32[]{:S(2)}, u32[]{:S(2)}) collective-permute-start(bf16[2,3,512,128]{3,2,1,0:T(8,128)(2,1)S(1)} %get-tuple-element.17), channel_id=1, source_target_pairs={{1,0},{2,1},{3,2},{4,3},{5,4},{6,5},{7,6},{8,7},{9,8},{10,9},{11,1... | collective-permute-start | bytes 2359304 | tf_op jit(solution)/shard_map/ppermute | solution.py:500
  35.9 0.0 copy-done.6
  36.0 0.7 select_bitcast_fusion.1
  36.7 0.1 copy.33
  36.8 0.1 copy.34
  36.9 0.0 copy-done.5
  36.9 0.0 copy-done.4
  36.9 0.6 maximum_bitcast_fusion.1.refs_4_.refs_10_
  37.5 0.6 pad_maximum_fusion.5.refs_5_.refs_11_
  38.1 31.7 %inner_columns.1 = (f32[2,16,512,128]{3,2,1,0:T(8,128)}, f32[2,16,8,512]{3,2,1,0:T(8,128)}, f32[2,8,512,128]{3,2,1,0:T(8,128)}) custom-call(bf16[2,16,512,128]{3,2,1,0:T(8,128)(2,1)} %refs_6_.1, f32[22,8,512]{2,1,0:T(8,128)} %get-tuple-element.18.refs_1_.refs_7_, s32[16,512]{1,0:T(8,128)} %refs_8_.1, s32[16,512]{1,0:T(8,128)} %refs_9_.1, ...), custom_call_target="tpu_custom_call" | custom-call | flops 83886080 | bytes 12582912 | tf_op jit(solution)/shard_map/inner_columns/pallas_call | solution.py:395
  69.8 0.6 add_convert_fusion.refs_0_
  70.5 0.7 slice_select_fusion.1
  71.1 0.0 copy-done.3
  71.2 0.0 copy-done.2
  71.2 0.7 fusion.8.base
  71.9 0.0 collective-permute-done.refs_2_
  71.9 0.0 copy-start
  71.9 0.0 collective-permute-done.1.refs_3_
  71.9 0.0 copy-start.1
  71.9 0.9 copy-done
  72.8 0.3 copy-done.1
  73.1 0.0 copy-start.7
  73.1 17.2 %edge_columns.1 = (f32[2,16,512,128]{3,2,1,0:T(8,128)}, f32[2,16,8,512]{3,2,1,0:T(8,128)}) custom-call(s32[4]{0:T(128)} %add_convert_fusion.refs_0_, f32[2,3,8,512]{3,2,1,0:T(8,128)} %get-tuple-element.14.refs_1_, bf16[2,3,512,128]{3,2,1,0:T(8,128)(2,1)} %copy-done, ...), custom_call_target="tpu_custom_call", output_to_operand_aliasing={{0}: (12, {}), {1}: (13, {})} | custom-call | flops 36700160 | bytes 5505024 | tf_op jit(solution)/shard_map/edge_columns/pallas_call | solution.py:395
  90.3 0.0 copy-done.7
  90.3 1.4 %fusion.4 = (f32[16,512]{1,0:T(8,128)S(1)}, f32[16,512]{1,0:T(8,128)S(1)}) fusion(f32[2,16,8,512]{3,2,1,0:T(8,128)} %get-tuple-element.24, f32[16,512]{1,0:T(8,128)S(1)} %copy-done.3, f32[4]{0:T(128)S(1)} %copy-done.7, f32[16,512]{1,0:T(8,128)S(1)} %divide_exponential_fusion), kind=kLoop, calls=%fused_computation.8 | loop fusion | flops 245760 | bytes 524304 | tf_op jit(solution)/shard_map/reduce_sum | solution.py:433
  91.8 0.7 pad_maximum_fusion.4.heat
  92.5 7.1 %heat_return.1 = f32[2,64,128]{2,1,0:T(8,128)} custom-call(f32[16,2,512]{2,1,0:T(2,128)} %pad_maximum_fusion.4.heat, f32[2,64,128]{2,1,0:T(8,128)} %fusion.8.base), custom_call_target="tpu_custom_call" | custom-call | tf_op jit(solution)/shard_map/heat_return/pallas_call | solution.py:529
  99.7 1.5 %copy.40 = f32[2,64,128]{2,1,0:T(8,128)} copy(f32[2,64,128]{2,1,0:T(8,128)} %heat_return.1) | data formatting | bytes 131072
  (7 shorter events, 0.1 us)
Async XLA Ops:
  0.6 35.3 %copy-start.6 = (f32[24,128]{1,0:T(8,128)S(1)}, f32[24,128]{1,0:T(8,128)}, u32[]{:S(2)}) copy-start(f32[24,128]{1,0:T(8,128)} %param.24) | copy-start | bytes 36868
  0.6 36.2 %copy-start.5 = (bf16[128,64]{0,1:T(8,128)(2,1)S(1)}, bf16[128,64]{0,1:T(8,128)(2,1)}, u32[]{:S(2)}) copy-start(bf16[128,64]{0,1:T(8,128)(2,1)} %param.22) | copy-start | bytes 49156
  0.7 36.2 %copy-start.4 = (bf16[128,64]{0,1:T(8,128)(2,1)S(1)}, bf16[128,64]{0,1:T(8,128)(2,1)}, u32[]{:S(2)}) copy-start(bf16[128,64]{0,1:T(8,128)(2,1)} %param.23) | copy-start | bytes 49156
  6.1 65.1 %copy-start.2 = (f32[2,64,128]{2,1,0:T(8,128)S(1)}, f32[2,64,128]{2,1,0:T(8,128)}, u32[]{:S(2)}) copy-start(f32[2,64,128]{2,1,0:T(8,128)} %param.19) | copy-start | bytes 196612
  26.7 44.4 %copy-start.3 = (f32[16,512]{1,0:T(8,128)S(1)}, f32[16,512]{1,0:T(8,128)}, u32[]{:S(2)}) copy-start(f32[16,512]{1,0:T(8,128)} %get-tuple-element.23) | copy-start | bytes 98308
  26.7 45.2 %collective-permute-start = (bf16[2,3,512,128]{3,2,1,0:T(8,128)(2,1)S(1)}, bf16[2,3,512,128]{3,2,1,0:T(8,128)(2,1)S(1)}, u32[]{:S(2)}, u32[]{:S(2)}) collective-permute-start(bf16[2,3,512,128]{3,2,1,0:T(8,128)(2,1)S(1)} %get-tuple-element.16), channel_id=1, source_target_pairs={{0,1},{1,2},{2,3},{3,4},{4,5},{5,6},{6,7},{7,8},{8,9},{9,10},{10,1... | collective-permute-start | bytes 2359304 | tf_op jit(solution)/shard_map/ppermute | solution.py:499
  28.9 43.0 %collective-permute-start.1 = (bf16[2,3,512,128]{3,2,1,0:T(8,128)(2,1)S(1)}, bf16[2,3,512,128]{3,2,1,0:T(8,128)(2,1)S(1)}, u32[]{:S(2)}, u32[]{:S(2)}) collective-permute-start(bf16[2,3,512,128]{3,2,1,0:T(8,128)(2,1)S(1)} %get-tuple-element.17), channel_id=1, source_target_pairs={{1,0},{2,1},{3,2},{4,3},{5,4},{6,5},{7,6},{8,7},{9,8},{10,9},{11,1... | collective-permute-start | bytes 2359304 | tf_op jit(solution)/shard_map/ppermute | solution.py:500
  71.9 0.9 copy-start
  71.9 1.2 %copy-start.1 = (bf16[2,3,512,128]{3,2,1,0:T(8,128)(2,1)}, bf16[2,3,512,128]{3,2,1,0:T(8,128)(2,1)S(1)}, u32[]{:S(2)}) copy-start(bf16[2,3,512,128]{3,2,1,0:T(8,128)(2,1)S(1)} %collective-permute-done.1.refs_3_) | copy-start | bytes 2359300
  73.1 17.2 %copy-start.7 = (f32[4]{0:T(128)S(1)}, f32[4]{0:T(128)}, u32[]{:S(2)}) copy-start(f32[4]{0:T(128)} %param.25) | copy-start | bytes 52

commit v4 on v3

--- a/solution.py
+++ b/solution.py
@@ -40,8 +40,8 @@
 
 def fields_kernel(
     gx_count, gy_count, width,
-    fields, sun, fringe,
-    strip, rim, strip_sun, fringe_in,
+    zonal, merid, moisture, depth, sun, fringe,
+    strip, rim, strip_sun, fringe_in, fields,
     send_a, recv_a, send_s, recv_s, send_r, recv_r, send_f, recv_f,
 ):
     gx = lax.axis_index("gx")
@@ -53,6 +53,13 @@
     left = lax.rem(gx + gx_count - 1, gx_count)
     up = lax.rem(gy + 1, gy_count)
     down = lax.rem(gy + gy_count - 1, gy_count)
+    margin = jnp.zeros((SUB,) + fields.shape[1:], jnp.float32)
+    fields[pl.ds(0, SUB)] = margin
+    fields[pl.ds(SUB + tile_x, SUB)] = margin
+    levels = zonal.shape[0]
+    for k, field in enumerate((zonal, merid, moisture, depth)):
+        for level in range(levels):
+            fields[pl.ds(SUB, tile_x), k * levels + level, :] = field[level]
     greet(gx_count, gy_count, 1)
     mine = pl.ds(pl.multiple_of(gy * tile_y, tile_y), tile_y)
 
@@ -151,11 +158,28 @@
 
 
 def return_kernel(
-    gx_count, gy_count, width, heat, base, out, tile, send_sem, recv_sem
+    gx_count, gy_count, width,
+    optical, sun, light, base, out, heat, tile, send_sem, recv_sem,
 ):
     gx = lax.axis_index("gx")
     gy = lax.axis_index("gy")
     tile_y = base.shape[2]
+
+    def radiate(x, carry):
+        cosine = sun[pl.ds(x, 1), :]
+        inverse = 1.0 / cosine
+        overhead = [jnp.zeros_like(cosine) for _ in range(NW)]
+        for level in reversed(range(optical.shape[0])):
+            warmth = jnp.zeros_like(cosine)
+            for w in range(NW):
+                transmitted = jnp.exp(-overhead[w] * inverse)
+                absorbed = optical[level, x, pl.ds(NW + w, 1), :]
+                warmth = warmth + light[w] * absorbed * transmitted
+                overhead[w] = overhead[w] + optical[level, x, pl.ds(w, 1), :]
+            heat[x, pl.ds(level, 1), :] = cosine * warmth
+        return carry
+
+    lax.fori_loop(0, width, radiate, 0)
     greet(gx_count, gy_count, 0)
 
     def slab(peer):
@@ -425,18 +449,6 @@
     )(*extras, *inputs, strip, bins, kinds, table, settle, *earlier)
 
 
-def radiate(optical, cosine, sunlight):
-    overhead = jnp.zeros_like(optical[0, :, :NW])
-    layers = [None] * optical.shape[0]
-    for height in reversed(range(optical.shape[0])):
-        transmitted = jnp.exp(-overhead / cosine[:, None])
-        layers[height] = cosine * jnp.sum(
-            sunlight[None, :, None] * optical[height, :, NW:] * transmitted, axis=1
-        )
-        overhead = overhead + optical[height, :, :NW]
-    return jnp.stack(layers, axis=1)
-
-
 def per_device(
     tracer_amounts,
     zonal_transit_ratio,
@@ -460,11 +472,7 @@
     gy = lax.axis_index("gy")
     tile_x, tile_y = sun_elevation_factor.shape
     both = ("gx", "gy")
-    fields = jnp.concatenate(
-        [zonal_transit_ratio, meridional_transit_ratio, moisture_ratio, stratum_depths], axis=0
-    )
-    field_count = fields.shape[0]
-    fields = jnp.pad(fields.transpose(1, 0, 2), ((SUB, SUB), (0, 0), (0, 0)))
+    field_count = 4 * levels
     t = thermal_anomaly
     span_y = max(tile_x, tile_y)
 
@@ -477,7 +485,7 @@
     dma = pltpu.SemaphoreType.DMA
     strip, rim, strip_sun, fringe_in = pl.pallas_call(
         functools.partial(fields_kernel, gx_count, gy_count, width),
-        in_specs=[VMEM_SPEC] * 3,
+        in_specs=[VMEM_SPEC] * 6,
         out_specs=[VMEM_SPEC] * 4,
         out_shape=[
             jax.ShapeDtypeStruct((width + 2 * SUB, field_count, ny), jnp.float32),
@@ -486,12 +494,16 @@
             jax.ShapeDtypeStruct(fringe.shape, jnp.float32),
         ],
         scratch_shapes=[
+            pltpu.VMEM((tile_x + 2 * SUB, field_count, tile_y), jnp.float32),
             dma((gy_count,)), dma((gy_count,)), dma((gy_count,)), dma((gy_count,)),
             dma((2,)), dma((gy_count,)), dma((4,)), dma((4,)),
         ],
         compiler_params=pltpu.CompilerParams(collective_id=0, has_side_effects=True),
         name="field_exchange",
-    )(fields, sun_elevation_factor, fringe)
+    )(
+        zonal_transit_ratio, meridional_transit_ratio, moisture_ratio, stratum_depths,
+        sun_elevation_factor, fringe,
+    )
 
     tail, head, strip = lax.optimization_barrier(
         (tracer_amounts[:, width - SUB :], tracer_amounts[:, :SUB], strip)
@@ -525,19 +537,19 @@
     updated, optical = chem_call(
         True, (flags, rim, halo_w, halo_e, saved), shared, (updated, optical)
     )
-    heat = radiate(optical, strip_sun, arriving_irradiance)
     anomaly = pl.pallas_call(
         functools.partial(return_kernel, gx_count, gy_count, width),
-        in_specs=[VMEM_SPEC] * 2,
+        in_specs=[VMEM_SPEC, VMEM_SPEC, SMEM_SPEC, VMEM_SPEC],
         out_specs=VMEM_SPEC,
         out_shape=jax.ShapeDtypeStruct(t.shape, jnp.float32),
         scratch_shapes=[
+            pltpu.VMEM((width, levels, ny), jnp.float32),
             pltpu.VMEM((tile_x, levels, tile_y), jnp.float32),
             dma((gy_count,)), dma((gy_count,)),
         ],
         compiler_params=pltpu.CompilerParams(collective_id=1, has_side_effects=True),
         name="heat_return",
-    )(heat, base)
+    )(optical, strip_sun, arriving_irradiance, base)
     return (updated, anomaly)
 
 

time: 102 us -> 97.2 us (0.953)
  local copies, waits for them, and re-layouts: 10.5 us -> 6.17 us
    unnamed x21 -> x7, local copies, waits for them, and re-layouts: 6.23 us -> 2.64 us
    reduce_sum x1 -> x0, other arithmetic: 1.43 us -> none  [radiate(): jnp.sum(sunlight[None, :, None] * optical[height, :, NW:] * transmitted,...]
  transfers between devices with their start and end apart: 2 -> 2, of which waited for: 0 -> 0; matrix products, arithmetic and copies ran while one was open for 4% -> 6% of each run, Pallas kernels for 31% -> 33%
where the time goes in v4:
time: 97.2 us; the launch traced here: 96.5 us
  Pallas kernels  74.4 us (77%)
  starting transfers between devices  9.16 us (9%)
  local copies, waits for them, and re-layouts  6.17 us (6%)
  other arithmetic  6.03 us (6%)
    pallas_call x2, Pallas kernels, chem_call(): pl.pallas_call(functools.partial(chem_kernel, levels, width, edge), grid=...  48.9 us
    pallas_call x1, Pallas kernels, per_device(): pl.pallas_call(functools.partial(fields_kernel, gx_count, gy_count, width...  17.8 us
    pallas_call x1, Pallas kernels, per_device(): pl.pallas_call(functools.partial(return_kernel, gx_count, gy_count, width...  7.75 us
    ppermute x1, starting transfers between devices, per_device(): halo_e = lax.ppermute(head, both, [(i + 1, i) for i in range(total - 1)])  7 us
    unnamed x7, local copies, waits for them, and re-layouts  2.64 us
    ppermute x1, starting transfers between devices, per_device(): halo_w = lax.ppermute(tail, both, [(i, i + 1) for i in range(total - 1)])  2.15 us
  transfers between devices with their start and end apart: 2, of which 0 were waited for; matrix products, arithmetic and copies ran while one was open for 6% of the time, Pallas kernels for 33%

profile of v4, /device:TPU:4, one launch (start us, length us, event | category | flops | bytes accessed | tf_op | source)
XLA Modules:
  0.0 96.5 jit_solution(2351361628319513208)
XLA Ops:
  0.6 1.1 %slice_reduce_fusion.1 = (f32[2,64]{1,0:T(2,128)S(1)}, f32[2,64]{1,0:T(2,128)S(1)}) fusion(f32[2,64,128]{2,1,0:T(8,128)} %param.19), kind=kLoop, calls=%fused_computation.11 | loop fusion | bytes 2048 | tf_op jit(solution)/shard_map/slice | solution.py:483
  1.7 0.7 fusion.8
  2.4 0.0 copy-start.2
  2.4 1.5 %fusion.7 = (bf16[2,3,512,128]{3,2,1,0:T(8,128)(2,1)S(1)}, bf16[2,3,512,128]{3,2,1,0:T(8,128)(2,1)S(1)}) fusion(bf16[2,16,512,128]{3,2,1,0:T(8,128)(2,1)} %refs_6_.1), kind=kLoop, calls=%fused_computation.29 | loop fusion | bytes 3145728 | tf_op jit(solution)/shard_map/slice | solution.py:509
  4.0 0.6 pad_maximum_fusion.5.fringe
  4.6 17.8 %field_exchange.1 = (f32[22,8,512]{2,1,0:T(8,128)}, f32[2,3,8,512]{3,2,1,0:T(8,128)}, f32[16,512]{1,0:T(8,128)}, f32[4,8,128]{2,1,0:T(8,128)}) custom-call(f32[2,64,128]{2,1,0:T(8,128)} %zonal.1, f32[2,64,128]{2,1,0:T(8,128)} %merid.1, f32[2,64,128]{2,1,0:T(8,128)} %moisture.1, f32[2,64,128]{2,1,0:T(8,128)} %depth.1, f32[64,128]{1,0:T(8,128)} %sun.1, ...), custom_call_target="tpu_custom_call" | custom-call | tf_op jit(solution)/shard_map/field_exchange/pallas_call | solution.py:486
  22.4 2.2 %collective-permute-start = (bf16[2,3,512,128]{3,2,1,0:T(8,128)(2,1)S(1)}, bf16[2,3,512,128]{3,2,1,0:T(8,128)(2,1)S(1)}, u32[]{:S(2)}, u32[]{:S(2)}) collective-permute-start(bf16[2,3,512,128]{3,2,1,0:T(8,128)(2,1)S(1)} %get-tuple-element.16), channel_id=1, source_target_pairs={{0,1},{1,2},{2,3},{3,4},{4,5},{5,6},{6,7},{7,8},{8,9},{9,10},{10,1... | collective-permute-start | bytes 2359304 | tf_op jit(solution)/shard_map/ppermute | solution.py:511
  24.5 7.0 %collective-permute-start.1 = (bf16[2,3,512,128]{3,2,1,0:T(8,128)(2,1)S(1)}, bf16[2,3,512,128]{3,2,1,0:T(8,128)(2,1)S(1)}, u32[]{:S(2)}, u32[]{:S(2)}) collective-permute-start(bf16[2,3,512,128]{3,2,1,0:T(8,128)(2,1)S(1)} %get-tuple-element.17), channel_id=1, source_target_pairs={{1,0},{2,1},{3,2},{4,3},{5,4},{6,5},{7,6},{8,7},{9,8},{10,9},{11,1... | collective-permute-start | bytes 2359304 | tf_op jit(solution)/shard_map/ppermute | solution.py:512
  31.6 0.7 reduce-precision_convert_fusion.1
  32.3 0.7 select_bitcast_fusion.1
  33.0 0.1 copy.25
  33.1 0.1 copy.26
  33.2 0.6 pad_maximum_fusion.4.refs_5_.refs_11_
  33.8 1.3 %maximum_bitcast_fusion.refs_4_.refs_10_ = bf16[128,128]{1,0:T(8,128)(2,1)} fusion(bf16[128,64]{0,1:T(8,128)(2,1)} %param.23, bf16[128,64]{0,1:T(8,128)(2,1)} %param.22), kind=kLoop, calls=%fused_computation.12 | loop fusion | flops 65536 | bytes 65536 | tf_op jit(solution)/shard_map/transpose | solution.py:523
  35.1 31.7 %inner_columns.1 = (f32[2,16,512,128]{3,2,1,0:T(8,128)}, f32[2,16,8,512]{3,2,1,0:T(8,128)}, f32[2,8,512,128]{3,2,1,0:T(8,128)}) custom-call(bf16[2,16,512,128]{3,2,1,0:T(8,128)(2,1)} %refs_6_.1, f32[22,8,512]{2,1,0:T(8,128)} %get-tuple-element.18.refs_1_.refs_7_, s32[16,512]{1,0:T(8,128)} %refs_8_.1, s32[16,512]{1,0:T(8,128)} %refs_9_.1, ...), custom_call_target="tpu_custom_call" | custom-call | flops 83886080 | bytes 12582912 | tf_op jit(solution)/shard_map/inner_columns/pallas_call | solution.py:419
  66.8 0.6 add_convert_fusion.refs_0_
  67.5 0.7 slice_select_fusion.1
  68.1 0.0 copy-done.2
  68.2 0.8 fusion.3.base
  68.9 0.0 collective-permute-done.refs_2_
  68.9 0.0 copy-start
  68.9 0.0 collective-permute-done.1.refs_3_
  68.9 0.0 copy-start.1
  68.9 0.9 copy-done
  69.8 0.3 copy-done.1
  70.1 17.2 %edge_columns.1 = (f32[2,16,512,128]{3,2,1,0:T(8,128)}, f32[2,16,8,512]{3,2,1,0:T(8,128)}) custom-call(s32[4]{0:T(128)} %add_convert_fusion.refs_0_, f32[2,3,8,512]{3,2,1,0:T(8,128)} %get-tuple-element.14.refs_1_, bf16[2,3,512,128]{3,2,1,0:T(8,128)(2,1)} %copy-done, ...), custom_call_target="tpu_custom_call", output_to_operand_aliasing={{0}: (12, {}), {1}: (13, {})} | custom-call | flops 36700160 | bytes 5505024 | tf_op jit(solution)/shard_map/edge_columns/pallas_call | solution.py:419
  87.3 7.7 %heat_return.1 = f32[2,64,128]{2,1,0:T(8,128)} custom-call(f32[2,16,8,512]{3,2,1,0:T(8,128)} %get-tuple-element.23.optical, f32[16,512]{1,0:T(8,128)} %get-tuple-element.24.sun, f32[4]{0:T(128)} %light.1, f32[2,64,128]{2,1,0:T(8,128)} %fusion.3.base), custom_call_target="tpu_custom_call" | custom-call | tf_op jit(solution)/shard_map/heat_return/pallas_call | solution.py:540
  95.1 1.5 %copy.32 = f32[2,64,128]{2,1,0:T(8,128)} copy(f32[2,64,128]{2,1,0:T(8,128)} %heat_return.1) | data formatting | bytes 131072
  (2 shorter events, 0.0 us)
Async XLA Ops:
  2.4 65.7 %copy-start.2 = (f32[2,64,128]{2,1,0:T(8,128)S(1)}, f32[2,64,128]{2,1,0:T(8,128)}, u32[]{:S(2)}) copy-start(f32[2,64,128]{2,1,0:T(8,128)} %param.19) | copy-start | bytes 196612
  22.4 46.6 %collective-permute-start = (bf16[2,3,512,128]{3,2,1,0:T(8,128)(2,1)S(1)}, bf16[2,3,512,128]{3,2,1,0:T(8,128)(2,1)S(1)}, u32[]{:S(2)}, u32[]{:S(2)}) collective-permute-start(bf16[2,3,512,128]{3,2,1,0:T(8,128)(2,1)S(1)} %get-tuple-element.16), channel_id=1, source_target_pairs={{0,1},{1,2},{2,3},{3,4},{4,5},{5,6},{6,7},{7,8},{8,9},{9,10},{10,1... | collective-permute-start | bytes 2359304 | tf_op jit(solution)/shard_map/ppermute | solution.py:511
  24.5 44.4 %collective-permute-start.1 = (bf16[2,3,512,128]{3,2,1,0:T(8,128)(2,1)S(1)}, bf16[2,3,512,128]{3,2,1,0:T(8,128)(2,1)S(1)}, u32[]{:S(2)}, u32[]{:S(2)}) collective-permute-start(bf16[2,3,512,128]{3,2,1,0:T(8,128)(2,1)S(1)} %get-tuple-element.17), channel_id=1, source_target_pairs={{1,0},{2,1},{3,2},{4,3},{5,4},{6,5},{7,6},{8,7},{9,8},{10,9},{11,1... | collective-permute-start | bytes 2359304 | tf_op jit(solution)/shard_map/ppermute | solution.py:512
  68.9 0.9 copy-start
  68.9 1.2 %copy-start.1 = (bf16[2,3,512,128]{3,2,1,0:T(8,128)(2,1)}, bf16[2,3,512,128]{3,2,1,0:T(8,128)(2,1)S(1)}, u32[]{:S(2)}) copy-start(bf16[2,3,512,128]{3,2,1,0:T(8,128)(2,1)S(1)} %collective-permute-done.1.refs_3_) | copy-start | bytes 2359300

commit v5 on v4

--- a/solution.py
+++ b/solution.py
@@ -41,7 +41,7 @@
 def fields_kernel(
     gx_count, gy_count, width,
     zonal, merid, moisture, depth, sun, fringe,
-    strip, rim, strip_sun, fringe_in, fields,
+    strip, rim, strip_sun, fringe_in, fields, landed,
     send_a, recv_a, send_s, recv_s, send_r, recv_r, send_f, recv_f,
 ):
     gx = lax.axis_index("gx")
@@ -77,7 +77,7 @@
     def slab(peer):
         return pltpu.make_async_remote_copy(
             src_ref=fields.at[pl.ds(peer * width, span)],
-            dst_ref=strip.at[:, :, mine],
+            dst_ref=landed.at[gy],
             send_sem=send_a.at[peer],
             recv_sem=recv_a.at[gy],
             device_id=(gx, peer),
@@ -129,7 +129,7 @@
             theirs = pl.ds(peer * tile_y, tile_y)
             pltpu.make_async_remote_copy(
                 src_ref=fields.at[pl.ds(0, span)],
-                dst_ref=strip.at[:, :, theirs],
+                dst_ref=landed.at[peer],
                 send_sem=send_a.at[peer],
                 recv_sem=recv_a.at[peer],
                 device_id=(gx, peer),
@@ -143,6 +143,7 @@
                 device_id=(gx, peer),
                 device_id_type=MESH,
             ).wait_recv()
+            strip[:, :, theirs] = landed[peer]
     for side, owner, source in ((0, 0, left), (1, gy_count - 1, right)):
         @pl.when(gy == owner)
         def _(side=side, source=source):
@@ -176,7 +177,9 @@
                 absorbed = optical[level, x, pl.ds(NW + w, 1), :]
                 warmth = warmth + light[w] * absorbed * transmitted
                 overhead[w] = overhead[w] + optical[level, x, pl.ds(w, 1), :]
-            heat[x, pl.ds(level, 1), :] = cosine * warmth
+            warmth = cosine * warmth
+            for peer in range(gy_count):
+                heat[peer, x, pl.ds(level, 1), :] = warmth[:, peer * tile_y : (peer + 1) * tile_y]
         return carry
 
     lax.fori_loop(0, width, radiate, 0)
@@ -184,7 +187,7 @@
 
     def slab(peer):
         return pltpu.make_async_remote_copy(
-            src_ref=heat.at[:, :, pl.ds(peer * tile_y, tile_y)],
+            src_ref=heat.at[peer],
             dst_ref=tile.at[pl.ds(gy * width, width)],
             send_sem=send_sem.at[peer],
             recv_sem=recv_sem.at[gy],
@@ -196,14 +199,13 @@
         @pl.when(gy != peer)
         def _(peer=peer):
             slab(peer).start()
-    mine = pl.ds(pl.multiple_of(gy * tile_y, tile_y), tile_y)
-    tile[pl.ds(gy * width, width)] = heat[:, :, mine]
+    tile[pl.ds(gy * width, width)] = heat[gy]
     for peer in range(gy_count):
         @pl.when(gy != peer)
         def _(peer=peer):
             slab(peer).wait_send()
             pltpu.make_async_remote_copy(
-                src_ref=heat.at[:, :, pl.ds(0, tile_y)],
+                src_ref=heat.at[peer],
                 dst_ref=tile.at[pl.ds(peer * width, width)],
                 send_sem=send_sem.at[peer],
                 recv_sem=recv_sem.at[peer],
@@ -495,6 +497,7 @@
         ],
         scratch_shapes=[
             pltpu.VMEM((tile_x + 2 * SUB, field_count, tile_y), jnp.float32),
+            pltpu.VMEM((gy_count, width + 2 * SUB, field_count, tile_y), jnp.float32),
             dma((gy_count,)), dma((gy_count,)), dma((gy_count,)), dma((gy_count,)),
             dma((2,)), dma((gy_count,)), dma((4,)), dma((4,)),
         ],
@@ -543,7 +546,7 @@
         out_specs=VMEM_SPEC,
         out_shape=jax.ShapeDtypeStruct(t.shape, jnp.float32),
         scratch_shapes=[
-            pltpu.VMEM((width, levels, ny), jnp.float32),
+            pltpu.VMEM((gy_count, width, levels, tile_y), jnp.float32),
             pltpu.VMEM((tile_x, levels, tile_y), jnp.float32),
             dma((gy_count,)), dma((gy_count,)),
         ],

time: 97.2 us -> 97.2 us (level)
  no operation moved by 1% of the time
where the time goes in v5:
time: 97.2 us; the launch traced here: 96.5 us
  Pallas kernels  74.4 us (77%)
  starting transfers between devices  9.16 us (9%)
  local copies, waits for them, and re-layouts  6.17 us (6%)
  other arithmetic  6.03 us (6%)
    pallas_call x2, Pallas kernels, chem_call(): pl.pallas_call(functools.partial(chem_kernel, levels, width, edge), grid=...  48.9 us
    pallas_call x1, Pallas kernels, per_device(): pl.pallas_call(functools.partial(fields_kernel, gx_count, gy_count, width...  17.8 us
    pallas_call x1, Pallas kernels, per_device(): pl.pallas_call(functools.partial(return_kernel, gx_count, gy_count, width...  7.75 us
    ppermute x1, starting transfers between devices, per_device(): halo_e = lax.ppermute(head, both, [(i + 1, i) for i in range(total - 1)])  6.97 us
    unnamed x7, local copies, waits for them, and re-layouts  2.64 us
    ppermute x1, starting transfers between devices, per_device(): halo_w = lax.ppermute(tail, both, [(i, i + 1) for i in range(total - 1)])  2.18 us
  transfers between devices with their start and end apart: 2, of which 0 were waited for; matrix products, arithmetic and copies ran while one was open for 6% of the time, Pallas kernels for 33%

profile of v5, /device:TPU:4, one launch (start us, length us, event | category | flops | bytes accessed | tf_op | source)
XLA Modules:
  0.0 96.5 jit_solution(7157900630119451278)
XLA Ops:
  0.6 1.1 %slice_reduce_fusion.1 = (f32[2,64]{1,0:T(2,128)S(1)}, f32[2,64]{1,0:T(2,128)S(1)}) fusion(f32[2,64,128]{2,1,0:T(8,128)} %param.19), kind=kLoop, calls=%fused_computation.11 | loop fusion | bytes 2048 | tf_op jit(solution)/shard_map/slice | solution.py:485
  1.7 0.7 fusion.8
  2.4 0.0 copy-start.2
  2.4 1.5 %fusion.7 = (bf16[2,3,512,128]{3,2,1,0:T(8,128)(2,1)S(1)}, bf16[2,3,512,128]{3,2,1,0:T(8,128)(2,1)S(1)}) fusion(bf16[2,16,512,128]{3,2,1,0:T(8,128)(2,1)} %refs_6_.1), kind=kLoop, calls=%fused_computation.29 | loop fusion | bytes 3145728 | tf_op jit(solution)/shard_map/slice | solution.py:512
  4.0 0.6 pad_maximum_fusion.5.fringe
  4.6 17.8 %field_exchange.1 = (f32[22,8,512]{2,1,0:T(8,128)}, f32[2,3,8,512]{3,2,1,0:T(8,128)}, f32[16,512]{1,0:T(8,128)}, f32[4,8,128]{2,1,0:T(8,128)}) custom-call(f32[2,64,128]{2,1,0:T(8,128)} %zonal.1, f32[2,64,128]{2,1,0:T(8,128)} %merid.1, f32[2,64,128]{2,1,0:T(8,128)} %moisture.1, f32[2,64,128]{2,1,0:T(8,128)} %depth.1, f32[64,128]{1,0:T(8,128)} %sun.1, ...), custom_call_target="tpu_custom_call" | custom-call | tf_op jit(solution)/shard_map/field_exchange/pallas_call | solution.py:488
  22.4 2.2 %collective-permute-start = (bf16[2,3,512,128]{3,2,1,0:T(8,128)(2,1)S(1)}, bf16[2,3,512,128]{3,2,1,0:T(8,128)(2,1)S(1)}, u32[]{:S(2)}, u32[]{:S(2)}) collective-permute-start(bf16[2,3,512,128]{3,2,1,0:T(8,128)(2,1)S(1)} %get-tuple-element.16), channel_id=1, source_target_pairs={{0,1},{1,2},{2,3},{3,4},{4,5},{5,6},{6,7},{7,8},{8,9},{9,10},{10,1... | collective-permute-start | bytes 2359304 | tf_op jit(solution)/shard_map/ppermute | solution.py:514
  24.5 7.0 %collective-permute-start.1 = (bf16[2,3,512,128]{3,2,1,0:T(8,128)(2,1)S(1)}, bf16[2,3,512,128]{3,2,1,0:T(8,128)(2,1)S(1)}, u32[]{:S(2)}, u32[]{:S(2)}) collective-permute-start(bf16[2,3,512,128]{3,2,1,0:T(8,128)(2,1)S(1)} %get-tuple-element.17), channel_id=1, source_target_pairs={{1,0},{2,1},{3,2},{4,3},{5,4},{6,5},{7,6},{8,7},{9,8},{10,9},{11,1... | collective-permute-start | bytes 2359304 | tf_op jit(solution)/shard_map/ppermute | solution.py:515
  31.6 0.7 reduce-precision_convert_fusion.1
  32.3 0.7 select_bitcast_fusion.1
  33.0 0.1 copy.25
  33.1 0.1 copy.26
  33.2 0.6 pad_maximum_fusion.4.refs_5_.refs_11_
  33.8 1.3 %maximum_bitcast_fusion.refs_4_.refs_10_ = bf16[128,128]{1,0:T(8,128)(2,1)} fusion(bf16[128,64]{0,1:T(8,128)(2,1)} %param.23, bf16[128,64]{0,1:T(8,128)(2,1)} %param.22), kind=kLoop, calls=%fused_computation.12 | loop fusion | flops 65536 | bytes 65536 | tf_op jit(solution)/shard_map/transpose | solution.py:526
  35.1 31.7 %inner_columns.1 = (f32[2,16,512,128]{3,2,1,0:T(8,128)}, f32[2,16,8,512]{3,2,1,0:T(8,128)}, f32[2,8,512,128]{3,2,1,0:T(8,128)}) custom-call(bf16[2,16,512,128]{3,2,1,0:T(8,128)(2,1)} %refs_6_.1, f32[22,8,512]{2,1,0:T(8,128)} %get-tuple-element.18.refs_1_.refs_7_, s32[16,512]{1,0:T(8,128)} %refs_8_.1, s32[16,512]{1,0:T(8,128)} %refs_9_.1, ...), custom_call_target="tpu_custom_call" | custom-call | flops 83886080 | bytes 12582912 | tf_op jit(solution)/shard_map/inner_columns/pallas_call | solution.py:421
  66.8 0.6 add_convert_fusion.refs_0_
  67.5 0.7 slice_select_fusion.1
  68.1 0.0 copy-done.2
  68.2 0.8 fusion.3.base
  68.9 0.0 collective-permute-done.refs_2_
  68.9 0.0 copy-start
  68.9 0.0 collective-permute-done.1.refs_3_
  68.9 0.0 copy-start.1
  68.9 0.9 copy-done
  69.8 0.3 copy-done.1
  70.1 17.2 %edge_columns.1 = (f32[2,16,512,128]{3,2,1,0:T(8,128)}, f32[2,16,8,512]{3,2,1,0:T(8,128)}) custom-call(s32[4]{0:T(128)} %add_convert_fusion.refs_0_, f32[2,3,8,512]{3,2,1,0:T(8,128)} %get-tuple-element.14.refs_1_, bf16[2,3,512,128]{3,2,1,0:T(8,128)(2,1)} %copy-done, ...), custom_call_target="tpu_custom_call", output_to_operand_aliasing={{0}: (12, {}), {1}: (13, {})} | custom-call | flops 36700160 | bytes 5505024 | tf_op jit(solution)/shard_map/edge_columns/pallas_call | solution.py:421
  87.3 7.7 %heat_return.1 = f32[2,64,128]{2,1,0:T(8,128)} custom-call(f32[2,16,8,512]{3,2,1,0:T(8,128)} %get-tuple-element.23.optical, f32[16,512]{1,0:T(8,128)} %get-tuple-element.24.sun, f32[4]{0:T(128)} %light.1, f32[2,64,128]{2,1,0:T(8,128)} %fusion.3.base), custom_call_target="tpu_custom_call" | custom-call | tf_op jit(solution)/shard_map/heat_return/pallas_call | solution.py:543
  95.1 1.5 %copy.32 = f32[2,64,128]{2,1,0:T(8,128)} copy(f32[2,64,128]{2,1,0:T(8,128)} %heat_return.1) | data formatting | bytes 131072
  (2 shorter events, 0.0 us)
Async XLA Ops:
  2.4 65.7 %copy-start.2 = (f32[2,64,128]{2,1,0:T(8,128)S(1)}, f32[2,64,128]{2,1,0:T(8,128)}, u32[]{:S(2)}) copy-start(f32[2,64,128]{2,1,0:T(8,128)} %param.19) | copy-start | bytes 196612
  22.4 46.6 %collective-permute-start = (bf16[2,3,512,128]{3,2,1,0:T(8,128)(2,1)S(1)}, bf16[2,3,512,128]{3,2,1,0:T(8,128)(2,1)S(1)}, u32[]{:S(2)}, u32[]{:S(2)}) collective-permute-start(bf16[2,3,512,128]{3,2,1,0:T(8,128)(2,1)S(1)} %get-tuple-element.16), channel_id=1, source_target_pairs={{0,1},{1,2},{2,3},{3,4},{4,5},{5,6},{6,7},{7,8},{8,9},{9,10},{10,1... | collective-permute-start | bytes 2359304 | tf_op jit(solution)/shard_map/ppermute | solution.py:514
  24.5 44.4 %collective-permute-start.1 = (bf16[2,3,512,128]{3,2,1,0:T(8,128)(2,1)S(1)}, bf16[2,3,512,128]{3,2,1,0:T(8,128)(2,1)S(1)}, u32[]{:S(2)}, u32[]{:S(2)}) collective-permute-start(bf16[2,3,512,128]{3,2,1,0:T(8,128)(2,1)S(1)} %get-tuple-element.17), channel_id=1, source_target_pairs={{1,0},{2,1},{3,2},{4,3},{5,4},{6,5},{7,6},{8,7},{9,8},{10,9},{11,1... | collective-permute-start | bytes 2359304 | tf_op jit(solution)/shard_map/ppermute | solution.py:515
  68.9 0.9 copy-start
  68.9 1.2 %copy-start.1 = (bf16[2,3,512,128]{3,2,1,0:T(8,128)(2,1)}, bf16[2,3,512,128]{3,2,1,0:T(8,128)(2,1)S(1)}, u32[]{:S(2)}) copy-start(bf16[2,3,512,128]{3,2,1,0:T(8,128)(2,1)S(1)} %collective-permute-done.1.refs_3_) | copy-start | bytes 2359300
